TPU v7x, 256 devices: a whole 4x4x8 slice. The times are simulated.
256 devices in a mesh: branch: 2 (over core), dap: 32 (over y, z), crop: 4 (over x).
Axes of the slice: x: 4, y: 4, z: 8, core: 2. Of those that a mesh axis runs over, the one named last changes fastest.
Arguments:
- homolog_features: bfloat16 [2048, 256, 256], P(('crop', 'dap')), parts along dimension 0, may hold values from -6 to 6
- alignment_mask: int32 [2048, 256], P(('crop', 'dap')), parts along dimension 0, may hold values 0 or 1
- residue_mask: int32 [1024], P('crop'), parts along dimension 0, may hold values from 0 to 1, as said below
- pairwise_state: bfloat16 [1024, 256, 128], P(('crop', 'dap')), parts along dimension 0, may hold values from -6 to 6
- vertical_gain_vector: float32 [256], replicated, may hold values from 0.25 to 1.75
- fourfold_projection_matrix: bfloat16 [256, 4, 8, 32], P(None, None, 'branch'), may hold values from -0.375 to 0.375
- mixing_projection_matrix: bfloat16 [8, 32, 256], P('branch'), may hold values from -0.375 to 0.375
- product_gain_vector: float32 [256], replicated, may hold values from 0.25 to 1.75
- product_source_matrix: bfloat16 [256, 32], P(None, 'branch'), may hold values from -0.375 to 0.375
- product_target_matrix: bfloat16 [256, 32], replicated, may hold values from -0.375 to 0.375
- outer_output_weight: bfloat16 [32, 32, 128], P('branch'), may hold values from -4 to 4
- triangle_norm_scale: float32 [128], replicated, may hold values from 0.25 to 1.75
- triangle_input_weight: bfloat16 [128, 4, 128], P(None, None, 'branch'), may hold values from -0.5 to 0.5
- triangle_gate_weight: bfloat16 [128, 128], P(None, 'branch'), may hold values from -0.5 to 0.5
- hidden_norm_scale: float32 [128], P('branch'), may hold values from 0.25 to 1.75
- triangle_output_weight: bfloat16 [128, 128], P('branch'), may hold values from -0.5 to 0.5
Outputs:
- homolog_mixed: bfloat16 [2048, 256, 256], P('crop', 'dap'), parts along dimension 0
- pairwise_output: bfloat16 [1024, 256, 128], P(('crop', 'dap'), None, 'branch'), parts along dimension 0
There are 4 independent parts, one for each index of `crop`. A program takes and returns all parts, laid end to end along the dimension named above; an argument that names none is the same for every part. Nothing has to cross between parts.
Inputs may be any that keep to these rules, and one draw needn't show every extreme that they name: residue_mask is 0 on a padded run at the crop's end of 1 to 65 residues, and 0 on some scattered unresolved residues before it; 1 elsewhere.
All inputs are finite; a program needn't handle non-finite values. No bound on the sum of `alignment_mask` on one device may be relied on, other than what follows from the above.
Results may differ from a plain program's by a relative error of at most 0.017.
Values may be sent and summed in bfloat16 or wider, within the bound.
A program may use at most 64 MiB of HBM per device.

v0:
```python
import jax
import jax.numpy as jnp
from jax import lax
from jax.sharding import PartitionSpec as P

eps_norm = 1e-05


def standardize_features(field, gain_vec):
    mean_val = jnp.mean(field, axis=-1, keepdims=True)
    variance = jnp.mean((field - mean_val) ** 2, axis=-1, keepdims=True)
    return (field - mean_val) * lax.rsqrt(variance + eps_norm) * gain_vec


def body(
    homolog_features,
    alignment_mask,
    residue_mask,
    pairwise_state,
    vertical_gain_vector,
    fourfold_projection_matrix,
    mixing_projection_matrix,
    product_gain_vector,
    product_source_matrix,
    product_target_matrix,
    outer_output_weight,
    triangle_norm_scale,
    triangle_input_weight,
    triangle_gate_weight,
    hidden_norm_scale,
    triangle_output_weight,
):
    group_count = lax.axis_size("dap")
    branches = lax.axis_size("branch")
    sequence_local, residue_total, alignment_width = homolog_features.shape
    residue_local = residue_total // group_count
    pair_width = pairwise_state.shape[2]
    residue_active = residue_mask.astype(jnp.float32)
    sequence_mask = (alignment_mask.astype(jnp.float32) * residue_active[None, :]).astype(
        jnp.bfloat16
    )
    local_heads = fourfold_projection_matrix.shape[2]
    head_width = fourfold_projection_matrix.shape[3]
    entering_matrix = fourfold_projection_matrix.reshape(
        alignment_width, 4 * local_heads * head_width
    )
    leaving_matrix = mixing_projection_matrix.reshape(local_heads * head_width, alignment_width)
    inv_root = 1.0 / head_width**0.5

    def single_column(operands):
        column_index, keep_mask = operands
        sequence_total = column_index.shape[0]
        normalized_input = standardize_features(
            column_index.astype(jnp.float32), vertical_gain_vector
        ).astype(jnp.bfloat16)
        projection = jnp.dot(
            normalized_input, entering_matrix, preferred_element_type=jnp.float32
        ).reshape(sequence_total, 4, local_heads, head_width)
        queries = projection[:, 0].astype(jnp.bfloat16)
        key_vecs = projection[:, 1].astype(jnp.bfloat16)
        values = projection[:, 2].astype(jnp.bfloat16)
        gating = jax.nn.sigmoid(projection[:, 3])
        scores = (
            jnp.einsum("shd,thd->hst", queries, key_vecs, preferred_element_type=jnp.float32)
            * inv_root
        )
        scores = jnp.where(
            (keep_mask.astype(jnp.float32) > 0.5)[None, None, :], scores, -1000000000.0
        )
        weights = jax.nn.softmax(scores, axis=-1).astype(jnp.bfloat16)
        attended = jnp.einsum("hst,thd->shd", weights, values, preferred_element_type=jnp.float32)
        gated_out = (
            (attended * gating)
            .astype(jnp.bfloat16)
            .reshape(sequence_total, local_heads * head_width)
        )
        return jnp.dot(gated_out, leaving_matrix, preferred_element_type=jnp.float32)

    stacked_blocks = homolog_features.reshape(
        sequence_local, group_count, residue_local, alignment_width
    )
    mask_stack = sequence_mask.reshape(sequence_local, group_count, residue_local)
    alignment_block = lax.all_to_all(stacked_blocks, "dap", split_axis=1, concat_axis=0, tiled=True)
    block_keep_flag = lax.all_to_all(mask_stack, "dap", split_axis=1, concat_axis=0, tiled=True)
    head_contributions = lax.map(
        single_column,
        (jnp.moveaxis(alignment_block[:, 0], 1, 0), jnp.moveaxis(block_keep_flag[:, 0], 1, 0)),
    )
    alignment_block, block_keep_flag, head_contributions = (
        alignment_block,
        block_keep_flag,
        jnp.moveaxis(head_contributions, 0, 1)[:, None],
    )
    alignment_unnormed = alignment_block[:, 0]
    keep_res = block_keep_flag[:, 0]
    head_contributions = head_contributions[:, 0]
    summed_blocks = lax.psum(head_contributions.astype(jnp.bfloat16), "branch").astype(jnp.float32)
    homolog_mixed = (alignment_unnormed.astype(jnp.float32) + summed_blocks).astype(jnp.bfloat16)
    sequence_total = homolog_mixed.shape[0]
    product_standardized = (
        standardize_features(homolog_mixed.astype(jnp.float32), product_gain_vector)
        .astype(jnp.bfloat16)
        .reshape(sequence_total * residue_local, alignment_width)
    )
    keep_float = keep_res.astype(jnp.float32)[..., None]
    left_panel = (
        jnp.dot(
            product_standardized, product_source_matrix, preferred_element_type=jnp.float32
        ).reshape(sequence_total, residue_local, -1)
        * keep_float
    ).astype(jnp.bfloat16)
    right_panel = (
        jnp.dot(
            product_standardized, product_target_matrix, preferred_element_type=jnp.float32
        ).reshape(sequence_total, residue_local, -1)
        * keep_float
    ).astype(jnp.bfloat16)
    left_flat = left_panel.reshape(sequence_total, -1)
    out_flat = outer_output_weight.reshape(-1, outer_output_weight.shape[2])
    right_rows, keep_rows = lax.all_gather((right_panel, keep_res), "dap", axis=1, tiled=True)
    piece_len = right_rows.shape[1]
    right_dim = right_rows.shape[2]
    outer_prod = lax.dot_general(
        left_flat,
        right_rows.reshape(sequence_total, piece_len * right_dim),
        (((0,), (0,)), ((), ())),
        preferred_element_type=jnp.float32,
    )
    outer_prod = (
        outer_prod.reshape(residue_local, -1, piece_len, right_dim)
        .transpose(0, 2, 1, 3)
        .reshape(residue_local, piece_len, -1)
        .astype(jnp.bfloat16)
    )
    update = jnp.dot(outer_prod, out_flat, preferred_element_type=jnp.float32)
    counts = lax.dot_general(
        keep_res, keep_rows, (((0,), (0,)), ((), ())), preferred_element_type=jnp.float32
    )
    opm_partial = update / jnp.maximum(counts, 1.0)[..., None]
    opm_update = lax.psum(opm_partial.astype(jnp.bfloat16), "branch").astype(jnp.float32)
    pair_mid = (pairwise_state.astype(jnp.float32) + opm_update).astype(jnp.bfloat16)
    pair_field = pair_mid.astype(jnp.float32)
    pair_normed = (
        standardize_features(pair_field, triangle_norm_scale)
        .astype(jnp.bfloat16)
        .reshape(residue_local * residue_total, pair_width)
    )
    hidden_loc = triangle_input_weight.shape[2]
    projection = jnp.dot(
        pair_normed,
        triangle_input_weight.reshape(pair_width, 4 * hidden_loc),
        preferred_element_type=jnp.float32,
    ).reshape(residue_local, residue_total, 4, hidden_loc)
    row_live = lax.dynamic_slice_in_dim(
        residue_active, lax.axis_index("dap") * residue_local, residue_local, 0
    )
    pair_live = (row_live[:, None] * residue_active[None, :])[..., None]
    tri_left = jnp.transpose(
        (pair_live * jax.nn.sigmoid(projection[:, :, 0]) * projection[:, :, 1]).astype(
            jnp.bfloat16
        ),
        (2, 0, 1),
    )
    tri_right = jnp.transpose(
        (pair_live * jax.nn.sigmoid(projection[:, :, 2]) * projection[:, :, 3]).astype(
            jnp.bfloat16
        ),
        (2, 0, 1),
    )
    tri_sum = jnp.einsum(
        "cik,cjk->cij",
        tri_left,
        lax.all_gather(tri_right, "dap", axis=1, tiled=True),
        preferred_element_type=jnp.float32,
    )
    moments = lax.psum((jnp.sum(tri_sum, axis=0), jnp.sum(tri_sum * tri_sum, axis=0)), "branch")
    hidden_all = hidden_loc * branches
    mean_val = moments[0] / hidden_all
    variance = moments[1] / hidden_all - mean_val * mean_val
    tri_scaled = (
        (tri_sum - mean_val[None])
        * lax.rsqrt(variance + eps_norm)[None]
        * hidden_norm_scale[:, None, None]
    ).astype(jnp.bfloat16)
    projected = lax.dot_general(
        tri_scaled,
        triangle_output_weight,
        (((0,), (0,)), ((), ())),
        preferred_element_type=jnp.float32,
    )
    update_part = lax.psum_scatter(
        projected.astype(jnp.bfloat16), "branch", scatter_dimension=2, tiled=True
    ).astype(jnp.float32)
    gating = jax.nn.sigmoid(
        jnp.dot(pair_normed, triangle_gate_weight, preferred_element_type=jnp.float32)
    ).reshape(residue_local, residue_total, -1)
    gate_width = gating.shape[2]
    pair_base = lax.dynamic_slice_in_dim(
        pair_field, lax.axis_index("branch") * gate_width, gate_width, 2
    )
    pairwise_output = (pair_base + gating * update_part).astype(jnp.bfloat16)
    return (homolog_mixed, pairwise_output)


def solution(mesh):
    in_specs = (
        P(("crop", "dap"), None, None),
        P(("crop", "dap"), None),
        P("crop"),
        P(("crop", "dap"), None, None),
        P(),
        P(None, None, "branch", None),
        P("branch", None, None),
        P(),
        P(None, "branch"),
        P(),
        P("branch", None, None),
        P(),
        P(None, None, "branch"),
        P(None, "branch"),
        P("branch"),
        P("branch", None),
    )
    out_specs = (P("crop", "dap", None), P(("crop", "dap"), None, "branch"))
    return jax.shard_map(body, mesh=mesh, in_specs=in_specs, out_specs=out_specs, check_vma=False)
```

profile of v0, /device:TPU:1, one launch (start us, length us, event | category | flops | bytes accessed | tf_op | source)
XLA Modules:
  0.0 599.4 jit_solution(18180345824477751055)
XLA Ops:
  9.9 12.0 %all-to-all-start.1 = ((bf16[16,32,8]{0,2,1:T(8,128)(2,1)}), bf16[16,32,8]{0,2,1:T(8,128)(2,1)S(1)}, u32[]{:S(2)}, u32[]{:S(2)}) async-start(bf16[16,32,8]{0,2,1:T(8,128)(2,1)} %bitcast.21), calls=%async_computation.1 | async-start | bytes 131072 | tf_op jit(solution)/shard_map/all_to_all | solution.py:84
  21.9 3.2 copy.73
  25.1 5.7 all-to-all-done.1
  30.8 4.0 all-to-all-start
  35.0 49.2 %all-to-all-done = bf16[16,32,8,256]{3,2,0,1:T(8,128)(2,1)S(1)} async-done(((bf16[16,32,8,256]{3,2,0,1:T(8,128)(2,1)}), bf16[16,32,8,256]{3,2,0,1:T(8,128)(2,1)S(1)}, u32[]{:S(2)}, u32[]{:S(2)}) %all-to-all-start) | async-done | bytes 2097184 | tf_op jit(solution)/shard_map/all_to_all | solution.py:83
  85.9 200.6 %while.10 = (s32[]{:T(128)}, bf16[8,512,256]{2,0,1:T(8,128)(2,1)}, bf16[8,512,256]{2,1,0:T(8,128)(2,1)}, f32[256]{0:T(256)S(1)}, bf16[256,512]{0,1:T(8,128)(2,1)...) while((s32[]{:T(128)}, bf16[8,512,256]{2,0,1:T(8,128)(2,1)}, ...), condition=%wide.region_5.6_spmd, body=%wide.region_0.5_spmd.sunk | while | flops 310315008 | bytes 13342317 | solution.py:85
  88.2 2.2 fusion.110
  90.5 5.2 fusion.111
  95.7 2.7 fusion.112
  99.0 12.0 %dynamic_update_slice.5 = bf16[8,512,256]{2,0,1:T(8,128)(2,1)} dynamic-update-slice(bf16[8,512,256]{2,0,1:T(8,128)(2,1)} %get-tuple-element.168, bf16[1,512,256]{2,0,1:T(2,128)(2,1)S(1)} %copy.129, s32[]{:T(128)} %get-tuple-element.167, s32[]{:T(128)} %constant.26.clone.1..sunk, s32[]{:T(128)} %constant.26.clone.1..sunk) | dynamic-update-slice | bytes 524292 | tf_op jit(solution)/shard_map/while/body/jit(dynamic_update_index_in_dim)/dynamic_update_slice | solution.py:85
  113.3 2.2 fusion.110
  115.6 5.2 fusion.111
  120.7 2.7 fusion.112
  124.1 12.0 %dynamic_update_slice.5 = bf16[8,512,256]{2,0,1:T(8,128)(2,1)} dynamic-update-slice(bf16[8,512,256]{2,0,1:T(8,128)(2,1)} %get-tuple-element.168, bf16[1,512,256]{2,0,1:T(2,128)(2,1)S(1)} %copy.129, s32[]{:T(128)} %get-tuple-element.167, s32[]{:T(128)} %constant.26.clone.1..sunk, s32[]{:T(128)} %constant.26.clone.1..sunk) | dynamic-update-slice | bytes 524292 | tf_op jit(solution)/shard_map/while/body/jit(dynamic_update_index_in_dim)/dynamic_update_slice | solution.py:85
  138.4 2.2 fusion.110
  140.7 5.2 fusion.111
  145.8 2.7 fusion.112
  149.1 12.0 %dynamic_update_slice.5 = bf16[8,512,256]{2,0,1:T(8,128)(2,1)} dynamic-update-slice(bf16[8,512,256]{2,0,1:T(8,128)(2,1)} %get-tuple-element.168, bf16[1,512,256]{2,0,1:T(2,128)(2,1)S(1)} %copy.129, s32[]{:T(128)} %get-tuple-element.167, s32[]{:T(128)} %constant.26.clone.1..sunk, s32[]{:T(128)} %constant.26.clone.1..sunk) | dynamic-update-slice | bytes 524292 | tf_op jit(solution)/shard_map/while/body/jit(dynamic_update_index_in_dim)/dynamic_update_slice | solution.py:85
  163.5 2.2 fusion.110
  165.7 5.2 fusion.111
  170.9 2.7 fusion.112
  174.2 12.0 %dynamic_update_slice.5 = bf16[8,512,256]{2,0,1:T(8,128)(2,1)} dynamic-update-slice(bf16[8,512,256]{2,0,1:T(8,128)(2,1)} %get-tuple-element.168, bf16[1,512,256]{2,0,1:T(2,128)(2,1)S(1)} %copy.129, s32[]{:T(128)} %get-tuple-element.167, s32[]{:T(128)} %constant.26.clone.1..sunk, s32[]{:T(128)} %constant.26.clone.1..sunk) | dynamic-update-slice | bytes 524292 | tf_op jit(solution)/shard_map/while/body/jit(dynamic_update_index_in_dim)/dynamic_update_slice | solution.py:85
  188.5 2.2 fusion.110
  190.8 5.2 fusion.111
  196.0 2.7 fusion.112
  199.3 12.0 %dynamic_update_slice.5 = bf16[8,512,256]{2,0,1:T(8,128)(2,1)} dynamic-update-slice(bf16[8,512,256]{2,0,1:T(8,128)(2,1)} %get-tuple-element.168, bf16[1,512,256]{2,0,1:T(2,128)(2,1)S(1)} %copy.129, s32[]{:T(128)} %get-tuple-element.167, s32[]{:T(128)} %constant.26.clone.1..sunk, s32[]{:T(128)} %constant.26.clone.1..sunk) | dynamic-update-slice | bytes 524292 | tf_op jit(solution)/shard_map/while/body/jit(dynamic_update_index_in_dim)/dynamic_update_slice | solution.py:85
  213.6 2.2 fusion.110
  215.9 5.2 fusion.111
  221.0 2.7 fusion.112
  224.4 12.0 %dynamic_update_slice.5 = bf16[8,512,256]{2,0,1:T(8,128)(2,1)} dynamic-update-slice(bf16[8,512,256]{2,0,1:T(8,128)(2,1)} %get-tuple-element.168, bf16[1,512,256]{2,0,1:T(2,128)(2,1)S(1)} %copy.129, s32[]{:T(128)} %get-tuple-element.167, s32[]{:T(128)} %constant.26.clone.1..sunk, s32[]{:T(128)} %constant.26.clone.1..sunk) | dynamic-update-slice | bytes 524292 | tf_op jit(solution)/shard_map/while/body/jit(dynamic_update_index_in_dim)/dynamic_update_slice | solution.py:85
  241.0 5.2 fusion.111
  246.1 2.7 fusion.112
  249.5 12.0 %dynamic_update_slice.5 = bf16[8,512,256]{2,0,1:T(8,128)(2,1)} dynamic-update-slice(bf16[8,512,256]{2,0,1:T(8,128)(2,1)} %get-tuple-element.168, bf16[1,512,256]{2,0,1:T(2,128)(2,1)S(1)} %copy.129, s32[]{:T(128)} %get-tuple-element.167, s32[]{:T(128)} %constant.26.clone.1..sunk, s32[]{:T(128)} %constant.26.clone.1..sunk) | dynamic-update-slice | bytes 524292 | tf_op jit(solution)/shard_map/while/body/jit(dynamic_update_index_in_dim)/dynamic_update_slice | solution.py:85
  263.8 2.2 fusion.110
  266.0 5.2 fusion.111
  271.2 2.7 fusion.112
  274.5 12.0 %dynamic_update_slice.5 = bf16[8,512,256]{2,0,1:T(8,128)(2,1)} dynamic-update-slice(bf16[8,512,256]{2,0,1:T(8,128)(2,1)} %get-tuple-element.168, bf16[1,512,256]{2,0,1:T(2,128)(2,1)S(1)} %copy.129, s32[]{:T(128)} %get-tuple-element.167, s32[]{:T(128)} %constant.26.clone.1..sunk, s32[]{:T(128)} %constant.26.clone.1..sunk) | dynamic-update-slice | bytes 524292 | tf_op jit(solution)/shard_map/while/body/jit(dynamic_update_index_in_dim)/dynamic_update_slice | solution.py:85
  286.8 31.3 %all-reduce.4.cloned.1.call-done = bf16[512,8,256]{2,1,0:T(8,128)(2,1)} async-done(((bf16[512,8,256]{2,1,0:T(8,128)(2,1)}), bf16[512,8,256]{2,1,0:T(8,128)(2,1)}) %all-reduce.4.cloned.1.call-update) | async-done | bytes 2097168 | tf_op jit(solution)/shard_map/psum | solution.py:97
  318.1 2.3 convert_reduce_fusion.1
  325.6 39.7 %all_gather.10 = bf16[512,256]{0,1:T(8,128)(2,1)S(1)} all-gather(bf16[512,8]{0,1:T(8,128)(2,1)S(1)} %bitcast.263), channel_id=1, replica_groups=mesh['branch'=2,'dap'=32,'crop'=4] {'dap'}, dimensions={1}, use_global_device_ids=true | all-gather | bytes 270336 | tf_op jit(solution)/shard_map/all_gather | solution.py:120
  365.5 3.1 multiply_convert_fusion.1
  369.2 55.2 %all-gather.3.cloned.1.call-done = bf16[512,256,32]{0,2,1:T(8,128)(2,1)} async-done(((bf16[512,8,32]{0,2,1:T(8,128)(2,1)}), bf16[512,256,32]{0,2,1:T(8,128)(2,1)}) %all-gather.3.cloned.1.call-update) | async-done | bytes 8388624 | tf_op jit(solution)/shard_map/all_gather | solution.py:120
  424.4 8.6 %fusion.32 = bf16[8,16,256,32]{2,1,3,0:T(8,128)(2,1)S(1)} fusion(bf16[256,32,512]{2,1,0:T(8,128)(2,1)} %bitcast.265, bf16[512,8,16]{0,2,1:T(8,128)(2,1)S(1)} %copy.79), kind=kOutput, calls=%fused_computation.44 | convolution fusion | flops 1073741824 | bytes 10616832 | tf_op jit(solution)/shard_map/dot_general | solution.py:123
  435.1 27.7 %all-reduce.6.cloned.1.call-done = bf16[8,256,128]{2,1,0:T(8,128)(2,1)} async-done(((bf16[8,256,128]{2,1,0:T(8,128)(2,1)}), bf16[8,256,128]{2,1,0:T(8,128)(2,1)}) %all-reduce.6.cloned.1.call-update) | async-done | bytes 524304 | tf_op jit(solution)/shard_map/psum | solution.py:140
  467.2 98.6 %all-gather.5.cloned.1.call-done = bf16[64,256,256]{2,0,1:T(8,128)(2,1)} async-done(((bf16[64,8,256]{2,0,1:T(8,128)(2,1)}), bf16[64,256,256]{2,0,1:T(8,128)(2,1)}) %all-gather.5.cloned.1.call-update) | async-done | bytes 8388624 | tf_op jit(solution)/shard_map/all_gather | solution.py:173
  565.8 8.0 %fusion.88 = (f32[8,256]{1,0:T(8,128)S(1)}, f32[8,256]{1,0:T(8,128)S(1)}, f32[64,8,256]{2,1,0:T(8,128)S(1)}) fusion(bf16[64,256,256]{2,0,1:T(8,128)(2,1)} %all-gather.5.cloned.1.call-done, bf16[64,8,256]{2,0,1:T(8,128)(2,1)S(1)} %get-tuple-element.102), kind=kOutput, calls=%fused_computation.120 | convolution fusion | flops 67497984 | bytes 9191424 | tf_op jit(solution)/shard_map/cik,cjk->cij/dot_general | solution.py:170
  573.8 4.2 all-reduce
  580.3 10.0 %reduce-scatter.2.cloned.1.call-done = bf16[8,256,64]{1,0,2:T(8,128)(2,1)} async-done(((bf16[8,256,128]{1,0,2:T(8,128)(2,1)}), bf16[8,256,64]{1,0,2:T(8,128)(2,1)}) %reduce-scatter.2.cloned.1.call-update) | async-done | bytes 262160 | tf_op jit(solution)/shard_map/reduce_scatter | solution.py:191
  (134 shorter events, 47.9 us)
Async XLA Ops:
  7.2 458.3 %copy-start = (bf16[128,4,64]{0,2,1:T(8,128)(2,1)S(1)}, bf16[128,4,64]{0,2,1:T(8,128)(2,1)}, u32[]{:S(2)}) copy-start(bf16[128,4,64]{0,2,1:T(8,128)(2,1)} %param.30) | copy-start | bytes 196612
  7.9 0.5 copy-start.7
  9.9 20.9 %all-to-all-start.1 = ((bf16[16,32,8]{0,2,1:T(8,128)(2,1)}), bf16[16,32,8]{0,2,1:T(8,128)(2,1)S(1)}, u32[]{:S(2)}, u32[]{:S(2)}) async-start(bf16[16,32,8]{0,2,1:T(8,128)(2,1)} %bitcast.21), calls=%async_computation.1 | async-start | bytes 131072 | tf_op jit(solution)/shard_map/all_to_all | solution.py:84
  25.1 60.8 %copy-start.2 = (bf16[256,4,4,32]{0,3,2,1:T(8,128)(2,1)S(1)}, bf16[256,4,4,32]{0,3,2,1:T(8,128)(2,1)}, u32[]{:S(2)}) copy-start(bf16[256,4,4,32]{0,3,2,1:T(8,128)(2,1)} %param.23) | copy-start | bytes 786436
  25.1 60.8 %copy-start.3 = (bf16[4,32,256]{2,1,0:T(8,128)(2,1)S(1)}, bf16[4,32,256]{2,1,0:T(8,128)(2,1)}, u32[]{:S(2)}) copy-start(bf16[4,32,256]{2,1,0:T(8,128)(2,1)} %param.24) | copy-start | bytes 196612
  25.1 60.8 %copy-start.5 = (f32[256]{0:T(256)S(1)}, f32[256]{0:T(256)}, u32[]{:S(2)}) copy-start(f32[256]{0:T(256)} %param.22) | copy-start | bytes 3076
  30.8 53.4 %all-to-all-start = ((bf16[16,32,8,256]{3,2,0,1:T(8,128)(2,1)}), bf16[16,32,8,256]{3,2,0,1:T(8,128)(2,1)S(1)}, u32[]{:S(2)}, u32[]{:S(2)}) async-start(bf16[16,32,8,256]{3,2,0,1:T(8,128)(2,1)} %copy.73), calls=%async_computation | async-start | bytes 4194304 | tf_op jit(solution)/shard_map/all_to_all | solution.py:83
  34.8 283.3 %all-reduce.4.cloned.1.call-start = ((), (), s32[]{:S(2)}) async-start(), calls=%async_computation.3 | async-start | bytes 4194304 | tf_op jit(solution)/shard_map/psum | solution.py:97
  286.6 137.9 %all-gather.3.cloned.1.call-start = ((), (), s32[]{:S(2)}) async-start(), calls=%async_computation.4 | async-start | bytes 8650752 | tf_op jit(solution)/shard_map/all_gather | solution.py:120
  318.0 4.1 copy-start.12
  318.1 4.1 copy-start.15
  320.3 1.7 copy-start.1
  322.1 43.3 %copy-start.14 = (bf16[256,16]{0,1:T(8,128)(2,1)S(1)}, bf16[256,16]{0,1:T(8,128)(2,1)}, u32[]{:S(2)}) copy-start(bf16[256,16]{0,1:T(8,128)(2,1)} %param.26) | copy-start | bytes 24580
  325.6 137.2 %all-reduce.6.cloned.1.call-start = ((), (), s32[]{:S(2)}) async-start(), calls=%async_computation.5 | async-start | bytes 1048576 | tf_op jit(solution)/shard_map/psum | solution.py:140
  424.4 8.7 %copy-start.11 = (bf16[16,32,128]{2,1,0:T(8,128)(2,1)S(1)}, bf16[16,32,128]{2,1,0:T(8,128)(2,1)}, u32[]{:S(2)}) copy-start(bf16[16,32,128]{2,1,0:T(8,128)(2,1)} %param.28) | copy-start | bytes 393220
  433.1 1.8 copy-start.8
  433.1 29.6 %copy-start.4 = (bf16[8,256,128]{2,1,0:T(8,128)(2,1)S(1)}, bf16[8,256,128]{2,1,0:T(8,128)(2,1)}, u32[]{:S(2)}) copy-start(bf16[8,256,128]{2,1,0:T(8,128)(2,1)} %param.21) | copy-start | bytes 1572868
  434.9 30.0 %copy-start.9 = (f32[128]{0:T(128)S(1)}, f32[128]{0:T(128)}, u32[]{:S(2)}) copy-start(f32[128]{0:T(128)} %param.29) | copy-start | bytes 1540
  434.9 130.9 %all-gather.5.cloned.1.call-start = ((), (), s32[]{:S(2)}) async-start(), calls=%async_computation.6 | async-start | bytes 8650752 | tf_op jit(solution)/shard_map/all_gather | solution.py:173
  466.9 123.4 %reduce-scatter.2.cloned.1.call-start = ((), (), s32[]{:S(2)}) async-start(), calls=%async_computation.7 | async-start | bytes 786432 | tf_op jit(solution)/shard_map/reduce_scatter | solution.py:191
  565.8 12.2 %copy-start.10 = (f32[64]{0:T(128)S(1)}, f32[64]{0:T(128)}, u32[]{:S(2)}) copy-start(f32[64]{0:T(128)} %param.32) | copy-start | bytes 772
  565.8 12.4 %copy-start.6 = (bf16[64,128]{1,0:T(8,128)(2,1)S(1)}, bf16[64,128]{1,0:T(8,128)(2,1)}, u32[]{:S(2)}) copy-start(bf16[64,128]{1,0:T(8,128)(2,1)} %param.33) | copy-start | bytes 49156
  565.8 13.9 %copy-start.13 = (bf16[128,64]{0,1:T(8,128)(2,1)S(1)}, bf16[128,64]{0,1:T(8,128)(2,1)}, u32[]{:S(2)}) copy-start(bf16[128,64]{0,1:T(8,128)(2,1)} %param.31) | copy-start | bytes 49156
Sparse Core Ops, SparseCore 0:
  286.7 31.3 all-reduce.3
  325.7 98.7 all-gather.2
  435.0 27.7 all-reduce.5
  467.1 98.6 all-gather.4
  579.8 10.5 reduce-scatter.1
where the time goes:
time: 603 us; the launch traced here: 599 us
  waiting for transfers between devices  278 us (46%)
  local copies, waits for them, and re-layouts  112 us (19%)
  matrix products  107 us (18%)
  blocking collectives  43.9 us (7%)
  other arithmetic  28.2 us (5%)
  starting transfers between devices  16.5 us (3%)
  between operations  14.1 us (2%)
    dynamic_update_slice x16, local copies, waits for them, and re-layouts, body(): lax.map(single_column, (jnp.moveaxis(alignment_block[:, 0], 1, 0), jnp.mo...  99.3 us
    all_gather x1, waiting for transfers between devices, body(): lax.all_gather(tri_right, 'dap', axis=1, tiled=True)  98.6 us
    all_gather x1, waiting for transfers between devices, body(): lax.all_gather((right_panel, keep_res), 'dap', axis=1, tiled=True)  55.2 us
    all_to_all x1, waiting for transfers between devices, body(): lax.all_to_all(stacked_blocks, 'dap', split_axis=1, concat_axis=0, tiled=...  49.2 us
    sub x8, matrix products, single_column(): weights = jax.nn.softmax(scores, axis=-1).astype(jnp.bfloat16)  41.3 us
    all_gather x1, blocking collectives, body(): lax.all_gather((right_panel, keep_res), 'dap', axis=1, tiled=True)  39.7 us
    psum x1, waiting for transfers between devices, body(): lax.psum(head_contributions.astype(jnp.bfloat16), 'branch')  31.3 us
    psum x1, waiting for transfers between devices, body(): lax.psum(opm_partial.astype(jnp.bfloat16), 'branch').astype(jnp.float32)  27.7 us
  transfers between devices with their start and end apart: 7, of which 7 were waited for; matrix products, arithmetic and copies ran while one was open for 1% of the time, Pallas kernels for 0%

commit v1 on v0

v1 whole, which is shorter than its diff:
```python
import functools

import jax
import jax.numpy as jnp
from jax import lax
from jax.experimental import pallas as pl
from jax.experimental.pallas import tpu as pltpu
from jax.sharding import PartitionSpec as P

eps_norm = 1e-05
SWAP = ((0, 1), (1, 0))
NT = (((1,), (1,)), ((), ()))
TN = (((0,), (0,)), ((), ()))


def standardize_features(field, gain_vec):
    mean_val = jnp.mean(field, axis=-1, keepdims=True)
    variance = jnp.mean((field - mean_val) ** 2, axis=-1, keepdims=True)
    return (field - mean_val) * lax.rsqrt(variance + eps_norm) * gain_vec


def sigmoid(x):
    return 1.0 / (1.0 + jnp.exp(-x))


def dot(a, b, dims):
    return lax.dot_general(a, b, dims, preferred_element_type=jnp.float32)


def column_kernel(
    heads, x_ref, mrow_ref, mcol_ref, gain_ref, w_ref, wo_ref, gain2_ref, wp_ref, mixed_ref, left_ref, right_ref,
    qkv_ref, gate_ref, gated_ref,
):
    width = x_ref.shape[-1]
    depth = mrow_ref.shape[-1]
    feats = wo_ref.shape[0]
    hd = feats // heads
    x = x_ref[:, 0].reshape(depth, width).astype(jnp.float32)
    n = standardize_features(x, gain_ref[...]).astype(jnp.bfloat16)
    proj = dot(w_ref[...], n, NT)
    for i in range(3):
        qkv_ref[i] = proj[i * feats : (i + 1) * feats].astype(jnp.bfloat16).reshape(heads, hd, depth)
    gate_ref[...] = sigmoid(proj[3 * feats :]).reshape(heads, hd, depth)
    live = mcol_ref[0] > 0.5
    inv_root = 1.0 / hd**0.5

    def one_head(h):
        scores = dot(qkv_ref[1, h], qkv_ref[0, h], TN) * inv_root
        scores = jnp.where(live, scores, -1000000000.0)
        e = jnp.exp(scores - jnp.max(scores, axis=0, keepdims=True))
        total = jnp.sum(e, axis=0, keepdims=True)
        att = jnp.dot(qkv_ref[2, h], e.astype(jnp.bfloat16), preferred_element_type=jnp.float32)
        gated_ref[h] = (att * (1.0 / total) * gate_ref[h]).astype(jnp.bfloat16)

    unroll = 4

    @pl.loop(0, heads // unroll)
    def _(step):
        for u in range(unroll):
            one_head(step * unroll + u)

    gated = gated_ref[...].reshape(feats, depth)
    mixed = (x + dot(gated, wo_ref[...], TN)).astype(jnp.bfloat16)
    mixed_ref[0] = mixed
    n2 = standardize_features(mixed.astype(jnp.float32), gain2_ref[...]).astype(jnp.bfloat16)
    panel = (dot(wp_ref[...], n2, NT) * mrow_ref[0]).astype(jnp.bfloat16)
    chans = left_ref.shape[1]
    left_ref[0] = panel[:chans]
    right_ref[0] = panel[chans:]


def column_stage(xs, mask_rows, gain, w_t, wo, gain2, wp_t, heads):
    groups, res, s_loc, width = xs.shape
    depth = groups * s_loc
    chans = wp_t.shape[0] // 2
    whole = lambda a: pl.BlockSpec(a.shape, lambda i: (0,) * a.ndim)
    mrow = mask_rows[:, None, :]
    mcol = mask_rows[:, :, None]
    return pl.pallas_call(
        functools.partial(column_kernel, heads),
        grid=(res,),
        in_specs=[
            pl.BlockSpec((groups, 1, s_loc, width), lambda i: (0, i, 0, 0)),
            pl.BlockSpec((1, 1, depth), lambda i: (i, 0, 0)),
            pl.BlockSpec((1, depth, 1), lambda i: (i, 0, 0)),
            whole(gain),
            whole(w_t),
            whole(wo),
            whole(gain2),
            whole(wp_t),
        ],
        out_specs=[
            pl.BlockSpec((1, depth, width), lambda i: (i, 0, 0)),
            pl.BlockSpec((1, chans, depth), lambda i: (i, 0, 0)),
            pl.BlockSpec((1, chans, depth), lambda i: (i, 0, 0)),
        ],
        out_shape=[
            jax.ShapeDtypeStruct((res, depth, width), jnp.bfloat16),
            jax.ShapeDtypeStruct((res, chans, depth), jnp.bfloat16),
            jax.ShapeDtypeStruct((res, chans, depth), jnp.bfloat16),
        ],
        scratch_shapes=[
            pltpu.VMEM((3, heads, wo.shape[0] // heads, depth), jnp.bfloat16),
            pltpu.VMEM((heads, wo.shape[0] // heads, depth), jnp.float32),
            pltpu.VMEM((heads, wo.shape[0] // heads, depth), jnp.bfloat16),
        ],
        name="column_attention",
    )(xs, mrow, mcol, gain, w_t, wo, gain2, wp_t)


def body(
    homolog_features,
    alignment_mask,
    residue_mask,
    pairwise_state,
    vertical_gain_vector,
    fourfold_projection_matrix,
    mixing_projection_matrix,
    product_gain_vector,
    product_source_matrix,
    product_target_matrix,
    outer_output_weight,
    triangle_norm_scale,
    triangle_input_weight,
    triangle_gate_weight,
    hidden_norm_scale,
    triangle_output_weight,
):
    f32, bf16 = jnp.float32, jnp.bfloat16
    groups = lax.axis_size("dap")
    me = lax.axis_index("dap")
    b = lax.axis_index("branch")
    s_loc, residues, width = homolog_features.shape
    res = residues // groups
    half = res // 2
    pair_width = pairwise_state.shape[2]

    def swap(a):
        return lax.ppermute(a, "branch", SWAP)

    def both(own, axis):
        other = swap(own)
        first = b == 0
        return jnp.concatenate([jnp.where(first, own, other), jnp.where(first, other, own)], axis=axis)

    def pick(a, axis, which):
        shape = a.shape
        a = a.reshape(shape[:axis] + (groups, 2, half) + shape[axis + 1 :])
        a = lax.dynamic_index_in_dim(a, which, axis + 1, keepdims=False)
        return a.reshape(shape[:axis] + (groups * half,) + shape[axis + 1 :])

    active = residue_mask.astype(f32)

    fourfold = both(fourfold_projection_matrix, 2)
    heads, hd = fourfold.shape[2:]
    feats = heads * hd
    w_t = fourfold.reshape(width, 4 * feats).T
    wo = both(mixing_projection_matrix.reshape(-1, width), 0)
    source = both(product_source_matrix, 1)
    chans = source.shape[1]
    wp_t = jnp.concatenate([source, product_target_matrix], axis=1).T
    outer_w = both(outer_output_weight, 0).reshape(chans * chans, pair_width)
    tri_in = both(triangle_input_weight, 2)
    hidden = tri_in.shape[2]
    tri_in = tri_in.reshape(pair_width, 4 * hidden)
    tri_gate = both(triangle_gate_weight, 1)
    hidden_gain = both(hidden_norm_scale, 0)
    tri_out = both(triangle_output_weight, 0)

    send = pick(homolog_features, 1, b).reshape(s_loc, groups, half, width).transpose(1, 2, 0, 3)
    xs = lax.all_to_all(send, "dap", split_axis=0, concat_axis=0, tiled=True)
    mask_all = lax.all_gather(alignment_mask.astype(bf16), "dap", axis=0, tiled=True)
    mask_t = (mask_all.astype(f32) * active[None, :]).T
    rows_t = lax.dynamic_slice_in_dim(mask_t, me * res, res, 0)
    own_t = lax.dynamic_slice_in_dim(mask_t, me * res + b * half, half, 0)

    mixed, left, right = column_stage(
        xs,
        own_t,
        vertical_gain_vector[None],
        w_t,
        wo,
        product_gain_vector[None],
        wp_t,
        heads,
    )
    depth = mixed.shape[1]
    left = both(left, 0).reshape(res * chans, depth)
    right = lax.all_gather(right.reshape(half * chans, depth), "dap", axis=0, tiled=True)
    homolog_mixed = both(mixed, 0).transpose(1, 0, 2)

    cols = groups * half
    outer = dot(left, right, NT).astype(bf16)
    outer = outer.reshape(res, chans, cols, chans).transpose(0, 2, 1, 3).reshape(res * cols, chans * chans)
    update = jnp.dot(outer, outer_w, preferred_element_type=f32).reshape(res, cols, pair_width)
    counts = dot(rows_t.astype(bf16), pick(mask_t, 0, b).astype(bf16), NT)
    update = update / jnp.maximum(counts, 1.0)[..., None]
    pair_mid = (pick(pairwise_state, 1, b).astype(f32) + update).astype(bf16)
    pair_field = pair_mid.astype(f32)
    pair_normed = standardize_features(pair_field, triangle_norm_scale).astype(bf16).reshape(res * cols, pair_width)
    proj = jnp.dot(pair_normed, tri_in, preferred_element_type=f32).reshape(res, cols, 4, hidden)
    row_live = lax.dynamic_slice_in_dim(active, me * res, res, 0)
    live = (row_live[:, None] * pick(active, 0, b)[None, :])[..., None]
    tri_left = (live * sigmoid(proj[:, :, 0]) * proj[:, :, 1]).astype(bf16)
    tri_right = (live * sigmoid(proj[:, :, 2]) * proj[:, :, 3]).astype(bf16)
    gate = sigmoid(jnp.dot(pair_normed, tri_gate, preferred_element_type=f32)).reshape(res, cols, pair_width)

    right_all = lax.all_gather(tri_right.transpose(0, 2, 1), "dap", axis=0, tiled=True)
    part = jnp.einsum("ick,jck->cij", tri_left.transpose(0, 2, 1), right_all, preferred_element_type=f32)
    tri_sum = pick(part, 2, b) + swap(pick(part, 2, 1 - b))
    mean_val = jnp.mean(tri_sum, axis=0, keepdims=True)
    variance = jnp.mean((tri_sum - mean_val) ** 2, axis=0, keepdims=True)
    tri_scaled = ((tri_sum - mean_val) * lax.rsqrt(variance + eps_norm) * hidden_gain[:, None, None]).astype(bf16)
    projected = dot(tri_scaled, tri_out, TN)
    out = (pair_field + gate * projected).astype(bf16)
    z_half = pair_width // 2
    own = lax.dynamic_slice_in_dim(out, b * z_half, z_half, 2)
    other = swap(lax.dynamic_slice_in_dim(out, (1 - b) * z_half, z_half, 2))
    own = own.reshape(res, groups, 1, half, z_half)
    other = other.reshape(res, groups, 1, half, z_half)
    first = b == 0
    out = jnp.concatenate([jnp.where(first, own, other), jnp.where(first, other, own)], axis=2)
    return (homolog_mixed, out.reshape(res, residues, z_half))


def solution(mesh):
    in_specs = (
        P(("crop", "dap"), None, None),
        P(("crop", "dap"), None),
        P("crop"),
        P(("crop", "dap"), None, None),
        P(),
        P(None, None, "branch", None),
        P("branch", None, None),
        P(),
        P(None, "branch"),
        P(),
        P("branch", None, None),
        P(),
        P(None, None, "branch"),
        P(None, "branch"),
        P("branch"),
        P("branch", None),
    )
    out_specs = (P("crop", "dap", None), P(("crop", "dap"), None, "branch"))
    return jax.shard_map(body, mesh=mesh, in_specs=in_specs, out_specs=out_specs, check_vma=False)
```

time: 603 us -> 356 us (0.59)
  waiting for transfers between devices: 278 us -> 168 us
  local copies, waits for them, and re-layouts: 112 us -> 28 us
  matrix products: 107 us -> 24.9 us
  Pallas kernels: 0 us -> 25.7 us
  other arithmetic: 28.2 us -> 8.05 us
  starting transfers between devices: 16.5 us -> 31.9 us
  blocking collectives: 43.9 us -> 54.6 us
    dynamic_update_slice x16 -> x0, local copies, waits for them, and re-layouts: 99.3 us -> none  [body(): lax.map(single_column, (jnp.moveaxis(alignment_block[:, 0], 1, 0), jnp.mo...]
    psum x2 -> x0, waiting for transfers between devices: 58.9 us -> none  [the longest x1 31.3 us: body(): lax.psum(head_contributions.astype(jnp.bfloat16), 'branch')]
    all_to_all x2 -> x1, waiting for transfers between devices: 54.8 us -> 0.01 us  [body(): xs = lax.all_to_all(send, 'dap', split_axis=0, concat_axis=0, tiled=True)]
    sub x8 -> x0, matrix products: 41.3 us -> none  [single_column(): weights = jax.nn.softmax(scores, axis=-1).astype(jnp.bfloat16)]
    dot_general x33 -> x7, matrix products: 65.8 us -> 24.9 us  [the longest x1 11.2 us: body(): jnp.einsum('ick,jck->cij', tri_left.transpose(0, 2, 1), right_all, prefer...]
    pallas_call x0 -> x1, Pallas kernels: none -> 25.7 us  [column_stage(): pl.pallas_call(functools.partial(column_kernel, heads), grid=(res,), in_s...]
    ppermute x0 -> x12, starting transfers between devices: none -> 19.8 us  [swap(): return lax.ppermute(a, 'branch', SWAP)]
    all_gather x1, blocking collectives: 39.7 us -> 54.6 us  [body(): lax.all_gather(alignment_mask.astype(bf16), 'dap', axis=0, tiled=True)]
  transfers between devices with their start and end apart: 7 -> 15, of which waited for: 7 -> 5; matrix products, arithmetic and copies ran while one was open for 1% -> 8% of each run, Pallas kernels for 0% -> 0%
where the time goes in v1:
time: 356 us
  waiting for transfers between devices  168 us (47%)
  blocking collectives  54.6 us (15%)
  starting transfers between devices  31.9 us (9%)
  local copies, waits for them, and re-layouts  28 us (8%)
  Pallas kernels  25.7 us (7%)
  matrix products  24.9 us (7%)
  between operations  14.6 us (4%)
  other arithmetic  8.05 us (2%)
    all_gather x1, waiting for transfers between devices, body(): lax.all_gather(tri_right.transpose(0, 2, 1), 'dap', axis=0, tiled=True)  92.3 us
    all_gather x1, waiting for transfers between devices, body(): lax.all_gather(right.reshape(half * chans, depth), 'dap', axis=0, tiled=T...  74.2 us
    all_gather x1, blocking collectives, body(): lax.all_gather(alignment_mask.astype(bf16), 'dap', axis=0, tiled=True)  54.6 us
    pallas_call x1, Pallas kernels, column_stage(): pl.pallas_call(functools.partial(column_kernel, heads), grid=(res,), in_s...  25.7 us
    ppermute x12, starting transfers between devices, swap(): return lax.ppermute(a, 'branch', SWAP)  19.8 us
    all_to_all x1, starting transfers between devices, body(): xs = lax.all_to_all(send, 'dap', split_axis=0, concat_axis=0, tiled=True)  12 us
    dot_general x1, matrix products, body(): jnp.einsum('ick,jck->cij', tri_left.transpose(0, 2, 1), right_all, prefer...  11.2 us
    reshape x1, local copies, waits for them, and re-layouts, body(): outer.reshape(res, chans, cols, chans).transpose(0, 2, 1, 3)  8.08 us
  transfers between devices with their start and end apart: 15, of which 5 were waited for; matrix products, arithmetic and copies ran while one was open for 8% of the time, Pallas kernels for 0%

profile of v1, /device:TPU:1, one launch (start us, length us, event | category | flops | bytes accessed | tf_op | source)
XLA Modules:
  0.0 355.6 jit_solution(3513504432177356666)
XLA Ops:
  7.2 2.6 reshape.188
  9.8 0.4 constant_dynamic-slice_fusion.4
  10.2 1.8 copy.157
  12.1 12.0 %all-to-all-start = ((bf16[32,4,16,256]{3,2,1,0:T(8,128)(2,1)}), bf16[32,4,16,256]{3,2,1,0:T(8,128)(2,1)S(1)}, u32[]{:S(2)}, u32[]{:S(2)}) async-start(bf16[32,4,16,256]{3,2,1,0:T(8,128)(2,1)} %bitcast.164), calls=%async_computation | async-start | bytes 2097152 | tf_op jit(solution)/shard_map/all_to_all | solution.py:171
  24.2 1.0 collective-permute-start
  25.3 0.4 collective-permute-start.2
  25.7 54.6 %all_gather.9 = bf16[512,256]{1,0:T(8,128)(2,1)S(1)} all-gather(bf16[16,256]{1,0:T(8,128)(2,1)S(1)} %convert_element_type.49), channel_id=1, replica_groups=mesh['branch'=2,'dap'=32,'crop'=4] {'dap'}, dimensions={0}, use_global_device_ids=true | all-gather | bytes 270336 | tf_op jit(solution)/shard_map/all_gather | solution.py:172
  80.7 1.3 copy.116.mcol_ref
  82.0 0.6 broadcast_in_dim.8.mrow_ref
  82.6 0.6 maximum_bitcast_fusion.5.wp_ref
  83.3 0.7 pad_maximum_fusion.3.wo_ref
  84.0 0.8 pad_maximum_fusion
  84.8 1.0 copy-done
  85.8 25.7 %column_attention.1 = (bf16[4,512,256]{2,1,0:T(8,128)(2,1)}, bf16[4,32,512]{2,1,0:T(8,128)(2,1)}, bf16[4,32,512]{2,1,0:T(8,128)(2,1)}) custom-call(bf16[32,4,16,256]{3,2,1,0:T(8,128)(2,1)} %copy-done, f32[4,1,512]{2,1,0:T(1,128)} %broadcast_in_dim.8.mrow_ref, f32[4,512,1]{2,1,0:T(8,128)} %copy.116.mcol_ref, f32[1,256]{1,0:T(1,128)} %bitcast.177, ...), custom_call_target="tpu_custom_call" | custom-call | tf_op jit(solution)/shard_map/column_attention/pallas_call | solution.py:79
  111.6 12.0 %collective-permute-start.5 = (bf16[16,32,128]{2,1,0:T(8,128)(2,1)S(1)}, bf16[16,32,128]{2,1,0:T(8,128)(2,1)S(1)}, u32[]{:S(2)}, u32[]{:S(2)}) collective-permute-start(bf16[16,32,128]{2,1,0:T(8,128)(2,1)S(1)} %copy-done.4), channel_id=1, source_target_pairs={{0,128},{128,0},{1,129},{129,1},{2,130},{130,2},{3,131},{131,3},{4... | collective-permute-start | bytes 393224 | tf_op jit(solution)/shard_map/ppermute | solution.py:139
  124.1 0.3 copy.117
  125.0 0.2 copy.119
  125.3 0.7 collective-permute-start.4
  126.0 1.0 collective-permute-done.4
  127.0 74.2 %all-gather.3.cloned.1.call-done = bf16[4096,512]{1,0:T(8,128)(2,1)} async-done(((bf16[128,512]{1,0:T(8,128)(2,1)}), bf16[4096,512]{1,0:T(8,128)(2,1)}) %all-gather.3.cloned.1.call-update) | async-done | bytes 4194320 | tf_op jit(solution)/shard_map/all_gather | solution.py:189
  201.2 3.5 convolution_convert_fusion
  204.7 8.1 %reshape.194 = bf16[8,32,128,32]{3,2,1,0:T(8,128)(2,1)} reshape(bf16[256,4096]{1,0:T(8,128)(2,1)S(1)} %convolution_convert_fusion) | data formatting | bytes 4194304 | tf_op jit(solution)/shard_map/reshape | solution.py:194
  212.7 6.2 %fusion.61 = (f32[8,128]{1,0:T(8,128)S(1)}, f32[8,128,128]{1,2,0:T(8,128)S(1)}) fusion(f32[8,128,128]{1,2,0:T(8,128)S(1)} %copy.119, f32[8,128]{1,0:T(8,128)S(1)} %convolution_maximum_fusion, bf16[16,32,128]{2,1,0:T(8,128)(2,1)S(1)} %get-tuple-element.33, bf16[16,32,128]{2,1,0:T(8,128)(2,1)S(1)} %get-tuple-element.32, bf16[8,32,128,32]{3,2,1,0:T(8,128)(2,1)} %reshape.194), kind=kOutput, calls=%fused_computation.113 | convolution fusion | flops 269220864 | bytes 3416064 | tf_op jit(solution)/shard_map/dot_general | solution.py:195
  219.2 0.5 fusion.42
  219.7 0.3 fusion.46
  220.0 0.9 copy.125
  220.9 3.4 collective-permute-start.9
  224.5 0.5 collective-permute-start.10
  225.2 0.3 collective-permute-start.3
  225.5 0.3 collective-permute-done.10
  225.9 0.6 broadcast_select_fusion.15
  226.7 92.3 %all-gather.5.cloned.1.call-done = bf16[256,128,128]{2,1,0:T(8,128)(2,1)} async-done(((bf16[8,128,128]{2,1,0:T(8,128)(2,1)}), bf16[256,128,128]{2,1,0:T(8,128)(2,1)}) %all-gather.5.cloned.1.call-update) | async-done | bytes 8388624 | tf_op jit(solution)/shard_map/all_gather | solution.py:208
  319.0 11.2 %fusion.2 = f32[128,8,256]{2,1,0:T(8,128)S(1)} fusion(bf16[8,128,128]{2,0,1:T(8,128)(2,1)S(1)} %copy.126, bf16[256,128,128]{2,1,0:T(8,128)(2,1)} %all-gather.5.cloned.1.call-done), kind=kOutput, calls=%fused_computation.2 | convolution fusion | flops 67108864 | bytes 9699328 | tf_op jit(solution)/shard_map/ick,jck->cij/dot_general | solution.py:209
  330.2 0.6 copy.128
  330.8 1.1 constant_dynamic-slice_fusion.1
  331.9 1.1 collective-permute-start.8
  333.0 1.7 broadcast_select_fusion.1
  334.7 0.9 copy.120
  335.5 2.1 fusion.9
  337.6 2.0 copy.137
  339.6 0.8 copy-done.1
  340.4 1.4 fusion.60
  342.0 0.4 multiply_reduce_fusion
  342.6 0.3 multiply_convert_fusion
  342.9 1.4 fusion.11
  344.6 2.5 copy.141
  347.4 0.2 copy.139
  347.8 1.0 copy.142
  (94 shorter events, 3.6 us)
Async XLA Ops:
  9.7 14.4 %copy-start.3 = (bf16[256,4,4,32]{0,3,2,1:T(8,128)(2,1)S(1)}, bf16[256,4,4,32]{0,3,2,1:T(8,128)(2,1)}, u32[]{:S(2)}) copy-start(bf16[256,4,4,32]{0,3,2,1:T(8,128)(2,1)} %param.21) | copy-start | bytes 786436
  9.7 15.5 %copy-start.6 = (bf16[4,32,256]{2,1,0:T(8,128)(2,1)S(1)}, bf16[4,32,256]{2,1,0:T(8,128)(2,1)}, u32[]{:S(2)}) copy-start(bf16[4,32,256]{2,1,0:T(8,128)(2,1)} %param.22) | copy-start | bytes 196612
  9.8 15.6 %copy-start.12 = (bf16[256,16]{0,1:T(8,128)(2,1)S(1)}, bf16[256,16]{0,1:T(8,128)(2,1)}, u32[]{:S(2)}) copy-start(bf16[256,16]{0,1:T(8,128)(2,1)} %param.24) | copy-start | bytes 24580
  9.8 16.0 %copy-start.13 = (s32[256]{0:T(256)S(1)}, s32[256]{0:T(256)}, u32[]{:S(2)}) copy-start(s32[256]{0:T(256)} %param.18) | copy-start | bytes 3076
  9.8 16.0 %copy-start.9 = (s32[16,256]{1,0:T(8,128)S(1)}, s32[16,256]{1,0:T(8,128)}, u32[]{:S(2)}) copy-start(s32[16,256]{1,0:T(8,128)} %param.17) | copy-start | bytes 49156
  9.8 72.8 %copy-start.10 = (bf16[256,32]{0,1:T(8,128)(2,1)S(1)}, bf16[256,32]{0,1:T(8,128)(2,1)}, u32[]{:S(2)}) copy-start(bf16[256,32]{0,1:T(8,128)(2,1)} %param.25) | copy-start | bytes 49156
  12.1 72.8 %all-to-all-start = ((bf16[32,4,16,256]{3,2,1,0:T(8,128)(2,1)}), bf16[32,4,16,256]{3,2,1,0:T(8,128)(2,1)S(1)}, u32[]{:S(2)}, u32[]{:S(2)}) async-start(bf16[32,4,16,256]{3,2,1,0:T(8,128)(2,1)} %bitcast.164), calls=%async_computation | async-start | bytes 2097152 | tf_op jit(solution)/shard_map/all_to_all | solution.py:171
  24.1 177.1 %all-gather.3.cloned.1.call-start = ((), (), s32[]{:S(2)}) async-start(), calls=%async_computation.1 | async-start | bytes 4325376 | tf_op jit(solution)/shard_map/all_gather | solution.py:189
  24.2 59.8 %collective-permute-start = (bf16[256,4,4,32]{0,3,2,1:T(8,128)(2,1)S(1)}, bf16[256,4,4,32]{0,3,2,1:T(8,128)(2,1)S(1)}, u32[]{:S(2)}, u32[]{:S(2)}) collective-permute-start(bf16[256,4,4,32]{0,3,2,1:T(8,128)(2,1)S(1)} %copy-done.3), channel_id=1, source_target_pairs={{0,128},{128,0},{1,129},{129,1},{2,130},{130,2},{3,131},{131,3},{4... | collective-permute-start | bytes 786440 | tf_op jit(solution)/shard_map/ppermute | solution.py:139
  25.2 58.0 %collective-permute-start.1 = (bf16[128,256]{1,0:T(8,128)(2,1)S(1)}, bf16[128,256]{1,0:T(8,128)(2,1)S(1)}, u32[]{:S(2)}, u32[]{:S(2)}) collective-permute-start(bf16[128,256]{1,0:T(8,128)(2,1)S(1)} %bitcast.176), channel_id=1, source_target_pairs={{0,128},{128,0},{1,129},{129,1},{2,130},{130,2},{3,131},{131,3},{4... | collective-permute-start | bytes 196616 | tf_op jit(solution)/shard_map/ppermute | solution.py:139
  25.3 57.3 %collective-permute-start.2 = (bf16[256,16]{0,1:T(8,128)(2,1)S(1)}, bf16[256,16]{0,1:T(8,128)(2,1)S(1)}, u32[]{:S(2)}, u32[]{:S(2)}) collective-permute-start(bf16[256,16]{0,1:T(8,128)(2,1)S(1)} %copy-done.12), channel_id=1, source_target_pairs={{0,128},{128,0},{1,129},{129,1},{2,130},{130,2},{3,131},{131,3},{4... | collective-permute-start | bytes 24584 | tf_op jit(solution)/shard_map/ppermute | solution.py:139
  25.7 85.9 %copy-start.4 = (bf16[16,32,128]{2,1,0:T(8,128)(2,1)S(1)}, bf16[16,32,128]{2,1,0:T(8,128)(2,1)}, u32[]{:S(2)}) copy-start(bf16[16,32,128]{2,1,0:T(8,128)(2,1)} %param.26) | copy-start | bytes 393220
  25.7 97.9 %copy-start.7 = (bf16[128,4,64]{0,2,1:T(8,128)(2,1)S(1)}, bf16[128,4,64]{0,2,1:T(8,128)(2,1)}, u32[]{:S(2)}) copy-start(bf16[128,4,64]{0,2,1:T(8,128)(2,1)} %param.28) | copy-start | bytes 196612
  80.6 43.5 %copy-start.2 = (bf16[8,256,128]{2,1,0:T(8,128)(2,1)S(1)}, bf16[8,256,128]{2,1,0:T(8,128)(2,1)}, u32[]{:S(2)}) copy-start(bf16[8,256,128]{2,1,0:T(8,128)(2,1)} %param.19) | copy-start | bytes 1572868
  84.8 1.0 copy-start
  111.5 13.7 %copy-start.5 = (bf16[4,32,512]{2,1,0:T(8,128)(2,1)S(1)}, bf16[4,32,512]{2,1,0:T(8,128)(2,1)}, u32[]{:S(2)}) copy-start(bf16[4,32,512]{2,1,0:T(8,128)(2,1)} %get-tuple-element.6) | copy-start | bytes 393220
  111.6 207.5 %all-gather.5.cloned.1.call-start = ((), (), s32[]{:S(2)}) async-start(), calls=%async_computation.2 | async-start | bytes 8650752 | tf_op jit(solution)/shard_map/all_gather | solution.py:208
  111.6 14.3 %collective-permute-start.5 = (bf16[16,32,128]{2,1,0:T(8,128)(2,1)S(1)}, bf16[16,32,128]{2,1,0:T(8,128)(2,1)S(1)}, u32[]{:S(2)}, u32[]{:S(2)}) collective-permute-start(bf16[16,32,128]{2,1,0:T(8,128)(2,1)S(1)} %copy-done.4), channel_id=1, source_target_pairs={{0,128},{128,0},{1,129},{129,1},{2,130},{130,2},{3,131},{131,3},{4... | collective-permute-start | bytes 393224 | tf_op jit(solution)/shard_map/ppermute | solution.py:139
  123.6 1.7 collective-permute-start.7
  125.3 1.7 collective-permute-start.4
  212.7 6.4 %copy-start.15 = (f32[128]{0:T(128)S(1)}, f32[128]{0:T(128)}, u32[]{:S(2)}) copy-start(f32[128]{0:T(128)} %param.27) | copy-start | bytes 1540
  219.0 1.9 copy-start.14
  219.0 5.3 %copy-start.11 = (bf16[128,64]{0,1:T(8,128)(2,1)S(1)}, bf16[128,64]{0,1:T(8,128)(2,1)}, u32[]{:S(2)}) copy-start(bf16[128,64]{0,1:T(8,128)(2,1)} %param.29) | copy-start | bytes 49156
  219.0 5.4 %copy-start.8 = (bf16[64,128]{1,0:T(8,128)(2,1)S(1)}, bf16[64,128]{1,0:T(8,128)(2,1)}, u32[]{:S(2)}) copy-start(bf16[64,128]{1,0:T(8,128)(2,1)} %param.31) | copy-start | bytes 49156
  220.9 4.2 %collective-permute-start.9 = (f32[64]{0:T(128)S(1)}, f32[64]{0:T(128)S(1)}, u32[]{:S(2)}, u32[]{:S(2)}) collective-permute-start(f32[64]{0:T(128)S(1)} %copy-done.14), channel_id=1, source_target_pairs={{0,128},{128,0},{1,129},{129,1},{2,130},{130,2},{3,131},{131,3},{4... | collective-permute-start | bytes 776 | tf_op jit(solution)/shard_map/ppermute | solution.py:139
  224.3 1.2 collective-permute-start.6
  224.5 1.4 collective-permute-start.10
  225.2 107.8 %collective-permute-start.3 = (bf16[4,512,256]{2,1,0:T(8,128)(2,1)}, bf16[4,512,256]{2,1,0:T(8,128)(2,1)}, u32[]{:S(2)}, u32[]{:S(2)}) collective-permute-start(bf16[4,512,256]{2,1,0:T(8,128)(2,1)} %get-tuple-element.5), channel_id=1, source_target_pairs={{0,128},{128,0},{1,129},{129,1},{2,130},{130,2},{3,131},{131,3},{4... | collective-permute-start | bytes 3145736 | tf_op jit(solution)/shard_map/ppermute | solution.py:139
  331.9 7.7 %collective-permute-start.8 = (f32[128,8,128]{0,1,2:T(8,128)}, f32[128,8,128]{0,1,2:T(8,128)S(1)}, u32[]{:S(2)}, u32[]{:S(2)}) collective-permute-start(f32[128,8,128]{0,1,2:T(8,128)} %bitcast.35), channel_id=1, source_target_pairs={{0,128},{128,0},{1,129},{129,1},{2,130},{130,2},{3,131},{131,3},{4... | collective-permute-start | bytes 1572872 | tf_op jit(solution)/shard_map/ppermute | solution.py:139
  339.6 0.8 copy-start.1
  344.3 2.8 collective-permute-start.11
Sparse Core Ops, SparseCore 0:
  111.7 89.4 all-gather.2
  221.0 97.9 all-gather.4

commit v2 on v1

--- a/solution.py
+++ b/solution.py
@@ -106,6 +106,161 @@
         ],
         name="column_attention",
     )(xs, mrow, mcol, gain, w_t, wo, gain2, wp_t)
+
+
+def remote(src, dst, send_sem, recv_sem, where):
+    return pltpu.make_async_remote_copy(
+        src_ref=src,
+        dst_ref=dst,
+        send_sem=send_sem,
+        recv_sem=recv_sem,
+        device_id=where,
+        device_id_type=pl.DeviceIdType.MESH,
+    )
+
+
+def greet(places):
+    barrier = pltpu.get_barrier_semaphore()
+    for where in places:
+        pl.semaphore_signal(barrier, inc=1, device_id=where, device_id_type=pl.DeviceIdType.MESH)
+    pl.semaphore_wait(barrier, len(places))
+
+
+def scatter_kernel(count, number, peer_of, slot_of, *refs):
+    ins, outs = refs[:number], refs[number : 2 * number]
+    send_sem, recv_sem, local_sem = refs[2 * number :]
+    me = slot_of(lax.axis_index("dap"))
+    greet([peer_of(lax.axis_index("dap"), d) for d in range(1, count)])
+    keeps = [pltpu.make_async_copy(a.at[me], o.at[me], local_sem.at[i]) for i, (a, o) in enumerate(zip(ins, outs))]
+    sends = []
+    for d in range(1, count):
+        place = peer_of(lax.axis_index("dap"), d)
+        target = slot_of(place["dap"])
+        for i, (a, o) in enumerate(zip(ins, outs)):
+            copy = remote(a.at[target], o.at[me], send_sem.at[i, d], recv_sem.at[i, d], place)
+            copy.start()
+            sends.append(copy)
+    for copy in keeps:
+        copy.start()
+    for d in range(1, count):
+        for i, (a, o) in enumerate(zip(ins, outs)):
+            source = lax.rem(me + count - d, count)
+            remote(a.at[source], o.at[source], send_sem.at[i, d], recv_sem.at[i, d], peer_of(lax.axis_index("dap"), d)).wait_recv()
+    for copy in sends:
+        copy.wait_send()
+    for copy in keeps:
+        copy.wait()
+
+
+def scatter(arrays, count, peer_of, slot_of, ident, name):
+    number = len(arrays)
+    return pl.pallas_call(
+        functools.partial(scatter_kernel, count, number, peer_of, slot_of),
+        in_specs=[pl.BlockSpec(memory_space=pl.ANY)] * number,
+        out_specs=[pl.BlockSpec(memory_space=pl.ANY)] * number,
+        out_shape=[jax.ShapeDtypeStruct(a.shape, a.dtype) for a in arrays],
+        scratch_shapes=[
+            pltpu.SemaphoreType.DMA((number, count)),
+            pltpu.SemaphoreType.DMA((number, count)),
+            pltpu.SemaphoreType.DMA((number,)),
+        ],
+        compiler_params=pltpu.CompilerParams(collective_id=ident, has_side_effects=True),
+        name=name,
+    )(*arrays)
+
+
+def block_kernel(
+    ny, nz, share, l_ref, r_ref, lg_ref, rg_ref, fsend, frecv, bsend, brecv, ysend, yrecv, ssend, srecv, local_sem
+):
+    me = lax.axis_index("dap")
+    core = lax.axis_index("branch")
+    y, z = me // nz, lax.rem(me, nz)
+    up = {"dap": y * nz + lax.rem(z + 1, nz)}
+    down = {"dap": y * nz + lax.rem(z + nz - 1, nz)}
+    column = [{"dap": lax.rem(y + d, ny) * nz + z} for d in range(1, ny)]
+    twin = {"branch": 1 - core}
+    greet([up, down] + column + ([twin] if share else []))
+    fwd, bwd = nz // 2, nz - 1 - nz // 2
+
+    def slot(which, place):
+        return lg_ref.at[which, place] if share else lg_ref.at[place]
+
+    def at(shift):
+        return lax.rem(z + nz + shift, nz)
+
+    def ahead(t):
+        return remote(l_ref if t == 0 else slot(core, at(-t)), slot(core, at(-t)), fsend.at[t], frecv.at[t], up)
+
+    def back(t):
+        return remote(l_ref if t == 0 else slot(core, at(t)), slot(core, at(t)), bsend.at[t], brecv.at[t], down)
+
+    def ahead_in(t):
+        return remote(l_ref, slot(core, at(-1 - t)), fsend.at[t], frecv.at[t], up)
+
+    def back_in(t):
+        return remote(l_ref, slot(core, at(1 + t)), bsend.at[t], brecv.at[t], down)
+
+    def pass_on(i, shift):
+        return remote(l_ref if shift == 0 else slot(core, at(shift)), slot(core, at(shift)), ssend.at[i], srecv.at[i], twin)
+
+    shifts = [0]
+    sends = [ahead(0)] + ([back(0)] if bwd else [])
+    sends += [remote(r_ref, rg_ref.at[y], ysend.at[d], yrecv.at[d], column[d]) for d in range(ny - 1)]
+    if share:
+        sends.append(pass_on(0, 0))
+    for copy in sends:
+        copy.start()
+    keeps = [
+        pltpu.make_async_copy(l_ref, slot(core, z), local_sem.at[0]),
+        pltpu.make_async_copy(r_ref, rg_ref.at[y], local_sem.at[1]),
+    ]
+    for copy in keeps:
+        copy.start()
+
+    def follow(copy):
+        copy.start()
+        sends.append(copy)
+
+    for t in range(fwd):
+        ahead_in(t).wait_recv()
+        if t + 1 < fwd:
+            follow(ahead(t + 1))
+        if share:
+            shifts.append(-1 - t)
+            follow(pass_on(len(shifts) - 1, -1 - t))
+        if t < bwd:
+            back_in(t).wait_recv()
+            if t + 1 < bwd:
+                follow(back(t + 1))
+            if share:
+                shifts.append(1 + t)
+                follow(pass_on(len(shifts) - 1, 1 + t))
+    for d in range(ny - 1):
+        remote(r_ref, rg_ref.at[lax.rem(y + ny - 1 - d, ny)], ysend.at[d], yrecv.at[d], column[d]).wait_recv()
+    if share:
+        for i, shift in enumerate(shifts):
+            remote(l_ref, slot(1 - core, at(shift)), ssend.at[i], srecv.at[i], twin).wait_recv()
+    for copy in sends:
+        copy.wait_send()
+    for copy in keeps:
+        copy.wait()
+
+
+def gather_blocks(left, right, ny, nz, share, ident, name):
+    sems = lambda n: pltpu.SemaphoreType.DMA((n,))
+    lead = (2, nz) if share else (nz,)
+    return pl.pallas_call(
+        functools.partial(block_kernel, ny, nz, share),
+        in_specs=[pl.BlockSpec(memory_space=pl.ANY)] * 2,
+        out_specs=[pl.BlockSpec(memory_space=pl.ANY)] * 2,
+        out_shape=[
+            jax.ShapeDtypeStruct(lead + left.shape, left.dtype),
+            jax.ShapeDtypeStruct((ny,) + right.shape, right.dtype),
+        ],
+        scratch_shapes=[sems(nz), sems(nz), sems(nz), sems(nz), sems(ny), sems(ny), sems(nz), sems(nz), sems(2)],
+        compiler_params=pltpu.CompilerParams(collective_id=ident, has_side_effects=True),
+        name=name,
+    )(left, right)
 
 
 def body(
@@ -167,12 +322,21 @@
     hidden_gain = both(hidden_norm_scale, 0)
     tri_out = both(triangle_output_weight, 0)
 
+    ny = 4 if groups % 16 == 0 else 2
+    nz = groups // ny
+    row = lambda i: i - lax.rem(i, nz)
+    row_peer = lambda i, d: {"dap": row(i) + lax.rem(lax.rem(i, nz) + d, nz)}
+    row_slot = lambda i: lax.rem(i, nz)
+    all_peer = lambda i, d: {"dap": lax.rem(i + d, groups)}
+
     send = pick(homolog_features, 1, b).reshape(s_loc, groups, half, width).transpose(1, 2, 0, 3)
-    xs = lax.all_to_all(send, "dap", split_axis=0, concat_axis=0, tiled=True)
-    mask_all = lax.all_gather(alignment_mask.astype(bf16), "dap", axis=0, tiled=True)
-    mask_t = (mask_all.astype(f32) * active[None, :]).T
-    rows_t = lax.dynamic_slice_in_dim(mask_t, me * res, res, 0)
-    own_t = lax.dynamic_slice_in_dim(mask_t, me * res + b * half, half, 0)
+    own_mask = pick(alignment_mask.astype(bf16), 1, b).reshape(s_loc, groups, half).transpose(1, 2, 0)
+    own_mask = jnp.pad(own_mask, ((0, 0), (0, 8 - half), (0, 128 - s_loc)))
+    xs, mask_in = scatter([send, own_mask], groups, all_peer, lambda i: i, 1, "feature_exchange")
+    depth = groups * s_loc
+    mask_in = mask_in[:, :half, :s_loc].transpose(1, 0, 2).reshape(half, depth).astype(f32)
+    own_active = lax.dynamic_slice_in_dim(active, me * res + b * half, half, 0)
+    own_t = mask_in * own_active[:, None]
 
     mixed, left, right = column_stage(
         xs,
@@ -184,43 +348,74 @@
         wp_t,
         heads,
     )
-    depth = mixed.shape[1]
-    left = both(left, 0).reshape(res * chans, depth)
-    right = lax.all_gather(right.reshape(half * chans, depth), "dap", axis=0, tiled=True)
+    tail = jnp.pad(own_t.astype(bf16), ((0, 8 - half), (0, 0)))
+    left = jnp.concatenate([left.reshape(half * chans, depth), tail], axis=0)
+    right = jnp.concatenate([right.reshape(half * chans, depth), tail], axis=0)
+    left, right = gather_blocks(left, right, ny, nz, True, 2, "panel_gather")
     homolog_mixed = both(mixed, 0).transpose(1, 0, 2)
 
+    panel_rows = half * chans
+    rows_i, cols_j = 2 * nz * half, ny * half
+    outer = dot(
+        left[:, :, :panel_rows].reshape(rows_i * chans, depth), right[:, :panel_rows].reshape(cols_j * chans, depth), NT
+    ).astype(bf16)
+    outer = outer.reshape(rows_i, chans, cols_j, chans).transpose(0, 2, 1, 3).reshape(rows_i * cols_j, chans * chans)
+    update = jnp.dot(outer, outer_w, preferred_element_type=f32).reshape(rows_i, cols_j, pair_width)
+    counts = dot(
+        left[:, :, panel_rows : panel_rows + half].reshape(rows_i, depth),
+        right[:, panel_rows : panel_rows + half].reshape(cols_j, depth),
+        NT,
+    )
+    update = (update / jnp.maximum(counts, 1.0)[..., None]).astype(bf16)
+    update = update.reshape(2, nz, half, cols_j, pair_width).transpose(1, 0, 2, 3, 4)
+    (update,) = scatter([update.reshape(nz, res, cols_j, pair_width)], nz, row_peer, row_slot, 3, "update_exchange")
+
+    def arrange(a):
+        a = a.reshape(a.shape[:1] + (ny, nz, 2, half) + a.shape[2:])
+        a = lax.dynamic_index_in_dim(a, b, 3, keepdims=False)
+        return jnp.swapaxes(a, 1, 2).reshape((a.shape[0], groups * half) + a.shape[4:])
+
     cols = groups * half
-    outer = dot(left, right, NT).astype(bf16)
-    outer = outer.reshape(res, chans, cols, chans).transpose(0, 2, 1, 3).reshape(res * cols, chans * chans)
-    update = jnp.dot(outer, outer_w, preferred_element_type=f32).reshape(res, cols, pair_width)
-    counts = dot(rows_t.astype(bf16), pick(mask_t, 0, b).astype(bf16), NT)
-    update = update / jnp.maximum(counts, 1.0)[..., None]
-    pair_mid = (pick(pairwise_state, 1, b).astype(f32) + update).astype(bf16)
+    update = update.transpose(1, 0, 2, 3).reshape(res, cols, pair_width).astype(f32)
+    pair_mid = (arrange(pairwise_state).astype(f32) + update).astype(bf16)
     pair_field = pair_mid.astype(f32)
     pair_normed = standardize_features(pair_field, triangle_norm_scale).astype(bf16).reshape(res * cols, pair_width)
     proj = jnp.dot(pair_normed, tri_in, preferred_element_type=f32).reshape(res, cols, 4, hidden)
     row_live = lax.dynamic_slice_in_dim(active, me * res, res, 0)
-    live = (row_live[:, None] * pick(active, 0, b)[None, :])[..., None]
+    live = (row_live[:, None] * arrange(active[None])[0][None, :])[..., None]
     tri_left = (live * sigmoid(proj[:, :, 0]) * proj[:, :, 1]).astype(bf16)
     tri_right = (live * sigmoid(proj[:, :, 2]) * proj[:, :, 3]).astype(bf16)
     gate = sigmoid(jnp.dot(pair_normed, tri_gate, preferred_element_type=f32)).reshape(res, cols, pair_width)
 
-    right_all = lax.all_gather(tri_right.transpose(0, 2, 1), "dap", axis=0, tiled=True)
-    part = jnp.einsum("ick,jck->cij", tri_left.transpose(0, 2, 1), right_all, preferred_element_type=f32)
-    tri_sum = pick(part, 2, b) + swap(pick(part, 2, 1 - b))
+    tri_left, tri_right = gather_blocks(
+        tri_left.transpose(2, 0, 1), tri_right.transpose(2, 0, 1), ny, nz, False, 4, "triangle_gather"
+    )
+    tri_left = tri_left.transpose(1, 0, 2, 3).reshape(hidden, nz * res, cols)
+    tri_right = tri_right.reshape(ny, hidden, 2, half, cols).transpose(2, 1, 0, 3, 4).reshape(2, hidden, cols_j, cols)
+
+    def share_of(which):
+        chosen = lax.dynamic_index_in_dim(tri_right, which, 0, keepdims=False)
+        return jnp.einsum("cik,cjk->cij", tri_left, chosen, preferred_element_type=f32)
+
+    given = swap(share_of(1 - b))
+    tri_sum = share_of(b) + given
     mean_val = jnp.mean(tri_sum, axis=0, keepdims=True)
     variance = jnp.mean((tri_sum - mean_val) ** 2, axis=0, keepdims=True)
     tri_scaled = ((tri_sum - mean_val) * lax.rsqrt(variance + eps_norm) * hidden_gain[:, None, None]).astype(bf16)
-    projected = dot(tri_scaled, tri_out, TN)
+    projected = dot(tri_scaled, tri_out, TN).astype(bf16)
+    (projected,) = scatter(
+        [projected.reshape(nz, res, cols_j, pair_width)], nz, row_peer, row_slot, 5, "triangle_exchange"
+    )
+    projected = projected.transpose(1, 0, 2, 3).reshape(res, cols, pair_width).astype(f32)
     out = (pair_field + gate * projected).astype(bf16)
     z_half = pair_width // 2
     own = lax.dynamic_slice_in_dim(out, b * z_half, z_half, 2)
     other = swap(lax.dynamic_slice_in_dim(out, (1 - b) * z_half, z_half, 2))
-    own = own.reshape(res, groups, 1, half, z_half)
-    other = other.reshape(res, groups, 1, half, z_half)
+    own = own.reshape(res, nz, ny, 1, half, z_half)
+    other = other.reshape(res, nz, ny, 1, half, z_half)
     first = b == 0
-    out = jnp.concatenate([jnp.where(first, own, other), jnp.where(first, other, own)], axis=2)
-    return (homolog_mixed, out.reshape(res, residues, z_half))
+    out = jnp.concatenate([jnp.where(first, own, other), jnp.where(first, other, own)], axis=3)
+    return (homolog_mixed, jnp.swapaxes(out, 1, 2).reshape(res, residues, z_half))
 
 
 def solution(mesh):

time: 356 us -> 220 us (0.62)
  waiting for transfers between devices: 168 us -> 1.42 us
  Pallas kernels: 25.7 us -> 135 us
  blocking collectives: 54.6 us -> 0 us
  starting transfers between devices: 31.9 us -> 11.2 us
  between operations: 14.6 us -> 1.29 us
  matrix products: 24.9 us -> 14.4 us
  other arithmetic: 8.05 us -> 18.4 us
  local copies, waits for them, and re-layouts: 28 us -> 37 us
    all_gather x2 -> x0, waiting for transfers between devices: 166 us -> none  [the longest x1 92.3 us: body(): lax.all_gather(tri_right.transpose(0, 2, 1), 'dap', axis=0, tiled=True)]
    pallas_call x0 -> x5, Pallas kernels: none -> 109 us  [the longest x3 58.8 us: scatter(): pl.pallas_call(functools.partial(scatter_kernel, count, number, peer_of,...]
    all_gather x1 -> x0, blocking collectives: 54.6 us -> none  [body(): lax.all_gather(alignment_mask.astype(bf16), 'dap', axis=0, tiled=True)]
    all_to_all x1 -> x0, starting transfers between devices: 12 us -> none  [body(): xs = lax.all_to_all(send, 'dap', split_axis=0, concat_axis=0, tiled=True)]
    ppermute x12 -> x11, starting transfers between devices: 19.8 us -> 11.2 us  [swap(): return lax.ppermute(a, 'branch', SWAP)]
    dot_general x1 -> x2, matrix products: 11.2 us -> 4.39 us  [share_of(): jnp.einsum('cik,cjk->cij', tri_left, chosen, preferred_element_type=f32)]
    slice x0 -> x5, local copies, waits for them, and re-layouts: none -> 5.87 us  [the longest x1 3.16 us: body(): left[:, :, :panel_rows].reshape(rows_i * chans, depth)]
    convert_element_type x1 -> x7, other arithmetic: 0.07 us -> 3.92 us  [the longest x1 1.04 us: body(): update.transpose(1, 0, 2, 3).reshape(res, cols, pair_width).astype(f32)]
  transfers between devices with their start and end apart: 15 -> 11, of which waited for: 5 -> 2; matrix products, arithmetic and copies ran while one was open for 8% -> 12% of each run, Pallas kernels for 0% -> 21%
where the time goes in v2:
time: 220 us; the launch traced here: 219 us
  Pallas kernels  135 us (61%)
  local copies, waits for them, and re-layouts  37 us (17%)
  other arithmetic  18.4 us (8%)
  matrix products  14.4 us (7%)
  starting transfers between devices  11.2 us (5%)
    pallas_call x3, Pallas kernels, scatter(): pl.pallas_call(functools.partial(scatter_kernel, count, number, peer_of,...  58.8 us
    pallas_call x2, Pallas kernels, gather_blocks(): pl.pallas_call(functools.partial(block_kernel, ny, nz, share), in_specs=[...  50.4 us
    pallas_call x1, Pallas kernels, column_stage(): pl.pallas_call(functools.partial(column_kernel, heads), grid=(res,), in_s...  25.7 us
    ppermute x11, starting transfers between devices, swap(): return lax.ppermute(a, 'branch', SWAP)  11.2 us
    unnamed x60, local copies, waits for them, and re-layouts  8.14 us
    reshape x1, local copies, waits for them, and re-layouts, body(): outer.reshape(rows_i, chans, cols_j, chans).transpose(0, 2, 1, 3)  7 us
    dot_general x1, matrix products, body(): jnp.dot(outer, outer_w, preferred_element_type=f32)  5.12 us
  transfers between devices with their start and end apart: 11, of which 2 were waited for; matrix products, arithmetic and copies ran while one was open for 12% of the time, Pallas kernels for 21%

profile of v2, /device:TPU:1, one launch (start us, length us, event | category | flops | bytes accessed | tf_op | source)
XLA Modules:
  0.0 218.8 jit_solution(8603967932826122552)
XLA Ops:
  0.6 3.3 %collective-permute-start = (bf16[256,4,4,32]{0,3,2,1:T(8,128)(2,1)}, bf16[256,4,4,32]{0,3,2,1:T(8,128)(2,1)S(1)}, u32[]{:S(2)}, u32[]{:S(2)}) collective-permute-start(bf16[256,4,4,32]{0,3,2,1:T(8,128)(2,1)} %param.21), channel_id=1, source_target_pairs={{0,128},{128,0},{1,129},{129,1},{2,130},{130,2},{3,131},{131,3},{4... | collective-permute-start | bytes 786440 | tf_op jit(solution)/shard_map/ppermute | solution.py:294
  5.0 2.5 %reshape.348 = bf16[16,32,2,4,256]{4,3,2,1,0:T(4,128)(2,1)S(1)} reshape(bf16[16,256,256]{2,1,0:T(8,128)(2,1)} %param.16) | data formatting | bytes 4194304 | tf_op jit(solution)/shard_map/reshape | solution.py:303
  8.0 1.8 copy.272
  10.0 0.7 pad.8.refs_1_
  10.6 34.6 %feature_exchange.1 = (bf16[32,4,16,256]{3,2,1,0:T(8,128)(2,1)}, bf16[32,8,128]{2,1,0:T(8,128)(2,1)}) custom-call(bf16[32,4,16,256]{3,2,1,0:T(8,128)(2,1)} %bitcast.166, bf16[32,8,128]{2,1,0:T(8,128)(2,1)} %pad.8.refs_1_), custom_call_target="tpu_custom_call" | custom-call | tf_op jit(solution)/shard_map/feature_exchange/pallas_call | solution.py:157
  45.2 0.8 convert_bitcast_fusion.3
  47.5 0.8 copy.194
  48.6 1.1 broadcast_multiply_fusion.mcol_ref
  49.7 0.7 broadcast_multiply_fusion.2.mrow_ref
  50.8 0.7 broadcast_multiply_fusion.4
  51.5 1.1 collective-permute-start.5
  52.6 0.6 pad_maximum_fusion.3
  55.9 0.7 pad_maximum_fusion.2.wo_ref
  56.5 1.6 broadcast_select_fusion.7
  58.2 0.8 pad_maximum_fusion
  59.1 25.7 %column_attention.1 = (bf16[4,512,256]{2,1,0:T(8,128)(2,1)}, bf16[4,32,512]{2,1,0:T(8,128)(2,1)}, bf16[4,32,512]{2,1,0:T(8,128)(2,1)}) custom-call(bf16[32,4,16,256]{3,2,1,0:T(8,128)(2,1)} %get-tuple-element.11.x_ref, f32[4,1,512]{2,1,0:T(1,128)} %broadcast_multiply_fusion.2.mrow_ref, f32[4,512,1]{2,1,0:T(8,128)} %broadcast_multiply_fusion.mcol_ref, ...), custom_call_target="tpu_custom_call" | custom-call | tf_op jit(solution)/shard_map/column_attention/pallas_call | solution.py:79
  84.8 1.7 fusion.45
  86.5 24.9 %panel_gather.1 = (bf16[2,8,136,512]{3,2,1,0:T(8,128)(2,1)}, bf16[4,136,512]{2,1,0:T(8,128)(2,1)}) custom-call(bf16[136,512]{1,0:T(8,128)(2,1)} %get-tuple-element.65.l_ref, bf16[136,512]{1,0:T(8,128)(2,1)} %get-tuple-element.64.r_ref), custom_call_target="tpu_custom_call" | custom-call | tf_op jit(solution)/shard_map/panel_gather/pallas_call | solution.py:252
  111.5 0.9 slice.30
  112.4 3.2 %slice.28 = bf16[2,8,128,512]{3,2,1,0:T(8,128)(2,1)} slice(bf16[2,8,136,512]{3,2,1,0:T(8,128)(2,1)} %get-tuple-element.16), slice={[0:2], [0:8], [0:128], [0:512]} | slice | bytes 4194304 | tf_op jit(solution)/shard_map/slice | solution.py:360
  115.6 0.9 slice.29
  116.6 0.7 copy.196
  117.3 3.0 %convolution_convert_fusion = bf16[2048,512]{1,0:T(8,128)(2,1)S(1)} fusion(bf16[2048,512]{1,0:T(8,128)(2,1)} %bitcast.169, bf16[512,512]{1,0:T(8,128)(2,1)} %bitcast.182), kind=kOutput, calls=%fused_computation.2 | convolution fusion | flops 1074790400 | bytes 4718592 | tf_op jit(solution)/shard_map/dot_general | solution.py:27
  120.3 7.0 %reshape.357 = bf16[64,32,16,32]{3,2,1,0:T(8,128)(2,1)} reshape(bf16[2048,512]{1,0:T(8,128)(2,1)S(1)} %convolution_convert_fusion) | data formatting | bytes 4194304 | tf_op jit(solution)/shard_map/reshape | solution.py:362
  127.3 5.1 %fusion.17 = bf16[64,16,128]{2,1,0:T(8,128)(2,1)S(1)} fusion(bf16[64,32,16,32]{3,2,1,0:T(8,128)(2,1)} %reshape.357, bf16[16,32,128]{2,1,0:T(8,128)(2,1)S(1)} %copy-done.10, bf16[16,32,128]{2,1,0:T(8,128)(2,1)S(1)} %copy-done.9, f32[64,16]{1,0:T(8,128)} %copy.196), kind=kOutput, calls=%fused_computation.23 | convolution fusion | flops 268828672 | bytes 2625536 | tf_op jit(solution)/shard_map/dot_general | solution.py:363
  132.4 0.7 copy.197
  133.1 12.9 %update_exchange.1 = bf16[8,8,16,128]{3,2,1,0:T(8,128)(2,1)} custom-call(bf16[8,8,16,128]{3,2,1,0:T(8,128)(2,1)} %bitcast.181), custom_call_target="tpu_custom_call" | custom-call | tf_op jit(solution)/shard_map/update_exchange/pallas_call | solution.py:157
  146.0 1.0 convert_bitcast_fusion.2
  149.6 0.9 fusion.60
  151.4 1.3 copy.241
  152.7 1.1 fusion.43
  153.8 25.5 %triangle_gather.1 = (bf16[8,128,8,128]{3,2,1,0:T(8,128)(2,1)}, bf16[4,128,8,128]{3,2,1,0:T(8,128)(2,1)}) custom-call(bf16[128,8,128]{2,1,0:T(8,128)(2,1)} %get-tuple-element.63.l_ref, bf16[128,8,128]{2,1,0:T(8,128)(2,1)} %get-tuple-element.62.r_ref), custom_call_target="tpu_custom_call" | custom-call | tf_op jit(solution)/shard_map/triangle_gather/pallas_call | solution.py:252
  179.3 1.6 copy.214
  180.9 0.9 constant_dynamic-slice_fusion.1
  181.8 2.2 %fusion.2 = f32[128,64,16]{1,2,0:T(8,128)} fusion(bf16[1,128,16,128]{3,1,2,0:T(8,128)(2,1)S(1)} %get-tuple-element.42, bf16[8,128,8,128]{3,2,1,0:T(8,128)(2,1)S(1)} %copy-done), kind=kOutput, calls=%fused_computation.4 | convolution fusion | flops 33554432 | bytes 3145728 | tf_op jit(solution)/shard_map/cik,cjk->cij/dot_general | solution.py:398
  184.0 2.5 %copy.217 = f32[128,64,16]{0,2,1:T(8,128)} copy(f32[128,64,16]{1,2,0:T(8,128)} %fusion.2) | data formatting | bytes 1048576 | tf_op jit(solution)/shard_map/cik,cjk->cij/dot_general | solution.py:398
  186.5 3.5 %collective-permute-start.7 = (f32[128,64,16]{0,2,1:T(8,128)}, f32[128,64,16]{0,2,1:T(8,128)}, u32[]{:S(2)}, u32[]{:S(2)}) collective-permute-start(f32[128,64,16]{0,2,1:T(8,128)} %copy.217), channel_id=1, source_target_pairs={{0,128},{128,0},{1,129},{129,1},{2,130},{130,2},{3,131},{131,3},{4... | collective-permute-start | bytes 1572872 | tf_op jit(solution)/shard_map/ppermute | solution.py:294
  190.6 2.2 %fusion.4 = f32[128,64,16]{1,2,0:T(8,128)} fusion(bf16[1,128,16,128]{3,1,2,0:T(8,128)(2,1)S(1)} %copy-done.2, bf16[8,128,8,128]{3,2,1,0:T(8,128)(2,1)S(1)} %copy-done), kind=kOutput, calls=%fused_computation.6 | convolution fusion | flops 33554432 | bytes 3145728 | tf_op jit(solution)/shard_map/cik,cjk->cij/dot_general | solution.py:398
  192.8 1.7 copy.218
  196.0 0.9 convolution_convert_fusion.1
  196.9 11.4 %triangle_exchange.1 = bf16[8,8,16,128]{3,2,1,0:T(8,128)(2,1)} custom-call(bf16[8,8,16,128]{3,2,1,0:T(8,128)(2,1)} %bitcast.180), custom_call_target="tpu_custom_call" | custom-call | tf_op jit(solution)/shard_map/triangle_exchange/pallas_call | solution.py:157
  208.3 1.0 convert_bitcast_fusion.1
  209.4 0.9 fusion.32
  210.4 1.7 collective-permute-start.10
  212.1 1.2 collective-permute-done.10
  213.7 1.0 copy.226
  214.7 1.4 broadcast_select_fusion.1
  216.3 2.5 %copy.225 = bf16[512,8,256]{2,1,0:T(8,128)(2,1)} copy(bf16[512,8,256]{2,0,1:T(8,128)(2,1)S(1)} %maximum_bitcast_fusion) | data formatting | bytes 4194304
  (130 shorter events, 12.5 us)
Async XLA Ops:
  0.6 57.6 %collective-permute-start = (bf16[256,4,4,32]{0,3,2,1:T(8,128)(2,1)}, bf16[256,4,4,32]{0,3,2,1:T(8,128)(2,1)S(1)}, u32[]{:S(2)}, u32[]{:S(2)}) collective-permute-start(bf16[256,4,4,32]{0,3,2,1:T(8,128)(2,1)} %param.21), channel_id=1, source_target_pairs={{0,128},{128,0},{1,129},{129,1},{2,130},{130,2},{3,131},{131,3},{4... | collective-permute-start | bytes 786440 | tf_op jit(solution)/shard_map/ppermute | solution.py:294
  4.0 51.9 %collective-permute-start.1 = (bf16[128,256]{1,0:T(8,128)(2,1)}, bf16[128,256]{1,0:T(8,128)(2,1)S(1)}, u32[]{:S(2)}, u32[]{:S(2)}) collective-permute-start(bf16[128,256]{1,0:T(8,128)(2,1)} %bitcast.188), channel_id=1, source_target_pairs={{0,128},{128,0},{1,129},{129,1},{2,130},{130,2},{3,131},{131,3},{4... | collective-permute-start | bytes 196616 | tf_op jit(solution)/shard_map/ppermute | solution.py:294
  4.1 49.2 %collective-permute-start.2 = (bf16[256,16]{0,1:T(8,128)(2,1)}, bf16[256,16]{0,1:T(8,128)(2,1)S(1)}, u32[]{:S(2)}, u32[]{:S(2)}) collective-permute-start(bf16[256,16]{0,1:T(8,128)(2,1)} %param.24), channel_id=1, source_target_pairs={{0,128},{128,0},{1,129},{129,1},{2,130},{130,2},{3,131},{131,3},{4... | collective-permute-start | bytes 24584 | tf_op jit(solution)/shard_map/ppermute | solution.py:294
  4.5 52.1 %collective-permute-start.4 = (bf16[16,32,128]{2,1,0:T(8,128)(2,1)}, bf16[16,32,128]{2,1,0:T(8,128)(2,1)}, u32[]{:S(2)}, u32[]{:S(2)}) collective-permute-start(bf16[16,32,128]{2,1,0:T(8,128)(2,1)} %param.26), channel_id=1, source_target_pairs={{0,128},{128,0},{1,129},{129,1},{2,130},{130,2},{3,131},{131,3},{4... | collective-permute-start | bytes 393224 | tf_op jit(solution)/shard_map/ppermute | solution.py:294
  4.6 46.9 %collective-permute-start.8 = (f32[64]{0:T(128)}, f32[64]{0:T(128)S(1)}, u32[]{:S(2)}, u32[]{:S(2)}) collective-permute-start(f32[64]{0:T(128)} %param.30), channel_id=1, source_target_pairs={{0,128},{128,0},{1,129},{129,1},{2,130},{130,2},{3,131},{131,3},{4... | collective-permute-start | bytes 776 | tf_op jit(solution)/shard_map/ppermute | solution.py:294
  7.5 2.3 %copy-start.15 = (s32[16,256]{1,0:T(8,128)S(1)}, s32[16,256]{1,0:T(8,128)}, u32[]{:S(2)}) copy-start(s32[16,256]{1,0:T(8,128)} %param.17) | copy-start | bytes 49156
  8.0 38.9 %copy-start.6 = (bf16[8,256,128]{2,1,0:T(8,128)(2,1)S(1)}, bf16[8,256,128]{2,1,0:T(8,128)(2,1)}, u32[]{:S(2)}) copy-start(bf16[8,256,128]{2,1,0:T(8,128)(2,1)} %param.19) | copy-start | bytes 1572868
  46.6 1.7 copy-start.22
  47.3 4.2 %copy-start.17 = (bf16[128,64]{0,1:T(8,128)(2,1)S(1)}, bf16[128,64]{0,1:T(8,128)(2,1)}, u32[]{:S(2)}) copy-start(bf16[128,64]{0,1:T(8,128)(2,1)} %param.29) | copy-start | bytes 49156
  47.3 5.3 %copy-start.24 = (f32[64]{0:T(128)S(1)}, f32[64]{0:T(128)}, u32[]{:S(2)}) copy-start(f32[64]{0:T(128)} %param.30) | copy-start | bytes 772
  47.3 6.0 %copy-start.13 = (bf16[128,4,64]{0,2,1:T(8,128)(2,1)S(1)}, bf16[128,4,64]{0,2,1:T(8,128)(2,1)}, u32[]{:S(2)}) copy-start(bf16[128,4,64]{0,2,1:T(8,128)(2,1)} %param.28) | copy-start | bytes 196612
  47.3 6.0 %copy-start.21 = (bf16[256,16]{0,1:T(8,128)(2,1)S(1)}, bf16[256,16]{0,1:T(8,128)(2,1)}, u32[]{:S(2)}) copy-start(bf16[256,16]{0,1:T(8,128)(2,1)} %param.24) | copy-start | bytes 24580
  47.3 6.0 %copy-start.16 = (bf16[256,32]{0,1:T(8,128)(2,1)S(1)}, bf16[256,32]{0,1:T(8,128)(2,1)}, u32[]{:S(2)}) copy-start(bf16[256,32]{0,1:T(8,128)(2,1)} %param.25) | copy-start | bytes 49156
  47.3 6.6 %copy-start.18 = (bf16[64,128]{1,0:T(8,128)(2,1)S(1)}, bf16[64,128]{1,0:T(8,128)(2,1)}, u32[]{:S(2)}) copy-start(bf16[64,128]{1,0:T(8,128)(2,1)} %param.31) | copy-start | bytes 49156
  47.3 8.5 %copy-start.12 = (bf16[4,32,256]{2,1,0:T(8,128)(2,1)S(1)}, bf16[4,32,256]{2,1,0:T(8,128)(2,1)}, u32[]{:S(2)}) copy-start(bf16[4,32,256]{2,1,0:T(8,128)(2,1)} %param.22) | copy-start | bytes 196612
  47.5 9.1 %copy-start.8 = (bf16[16,32,128]{2,1,0:T(8,128)(2,1)S(1)}, bf16[16,32,128]{2,1,0:T(8,128)(2,1)}, u32[]{:S(2)}) copy-start(bf16[16,32,128]{2,1,0:T(8,128)(2,1)} %param.26) | copy-start | bytes 393220
  48.3 9.9 %copy-start.7 = (bf16[256,4,4,32]{0,3,2,1:T(8,128)(2,1)S(1)}, bf16[256,4,4,32]{0,3,2,1:T(8,128)(2,1)}, u32[]{:S(2)}) copy-start(bf16[256,4,4,32]{0,3,2,1:T(8,128)(2,1)} %param.21) | copy-start | bytes 786436
  51.5 2.4 %collective-permute-start.5 = (bf16[128,64]{0,1:T(8,128)(2,1)S(1)}, bf16[128,64]{0,1:T(8,128)(2,1)S(1)}, u32[]{:S(2)}, u32[]{:S(2)}) collective-permute-start(bf16[128,64]{0,1:T(8,128)(2,1)S(1)} %copy-done.17), channel_id=1, source_target_pairs={{0,128},{128,0},{1,129},{129,1},{2,130},{130,2},{3,131},{131,3},{4... | collective-permute-start | bytes 49160 | tf_op jit(solution)/shard_map/ppermute | solution.py:294
  53.2 2.6 %collective-permute-start.6 = (bf16[128,4,64]{0,2,1:T(8,128)(2,1)S(1)}, bf16[128,4,64]{0,2,1:T(8,128)(2,1)S(1)}, u32[]{:S(2)}, u32[]{:S(2)}) collective-permute-start(bf16[128,4,64]{0,2,1:T(8,128)(2,1)S(1)} %copy-done.13), channel_id=1, source_target_pairs={{0,128},{128,0},{1,129},{129,1},{2,130},{130,2},{3,131},{131,3},{4... | collective-permute-start | bytes 196616 | tf_op jit(solution)/shard_map/ppermute | solution.py:294
  53.9 1.3 collective-permute-start.9
  112.4 3.2 %copy-start.5 = (bf16[4,136,512]{2,1,0:T(8,128)(2,1)S(1)}, bf16[4,136,512]{2,1,0:T(8,128)(2,1)}, u32[]{:S(2)}) copy-start(bf16[4,136,512]{2,1,0:T(8,128)(2,1)} %get-tuple-element.17) | copy-start | bytes 1671172
  120.3 7.0 %copy-start.9 = (bf16[16,32,128]{2,1,0:T(8,128)(2,1)S(1)}, bf16[16,32,128]{2,1,0:T(8,128)(2,1)}, u32[]{:S(2)}) copy-start(bf16[16,32,128]{2,1,0:T(8,128)(2,1)} %get-tuple-element.50) | copy-start | bytes 393220
  120.3 7.0 %copy-start.10 = (bf16[16,32,128]{2,1,0:T(8,128)(2,1)S(1)}, bf16[16,32,128]{2,1,0:T(8,128)(2,1)}, u32[]{:S(2)}) copy-start(bf16[16,32,128]{2,1,0:T(8,128)(2,1)} %get-tuple-element.51) | copy-start | bytes 393220
  146.0 2.8 %copy-start.25 = (f32[128]{0:T(128)S(1)}, f32[128]{0:T(128)}, u32[]{:S(2)}) copy-start(f32[128]{0:T(128)} %param.27) | copy-start | bytes 1540
  150.6 2.1 copy-start.14
  179.2 2.5 %copy-start = (bf16[8,128,8,128]{3,2,1,0:T(8,128)(2,1)S(1)}, bf16[8,128,8,128]{3,2,1,0:T(8,128)(2,1)}, u32[]{:S(2)}) copy-start(bf16[8,128,8,128]{3,2,1,0:T(8,128)(2,1)} %get-tuple-element.18) | copy-start | bytes 6291460
  184.0 6.1 %copy-start.19 = (bf16[128,64]{0,1:T(8,128)(2,1)S(1)}, bf16[128,64]{0,1:T(8,128)(2,1)}, u32[]{:S(2)}) copy-start(bf16[128,64]{0,1:T(8,128)(2,1)} %get-tuple-element.56) | copy-start | bytes 49156
  184.0 6.2 %copy-start.20 = (bf16[128,64]{0,1:T(8,128)(2,1)S(1)}, bf16[128,64]{0,1:T(8,128)(2,1)}, u32[]{:S(2)}) copy-start(bf16[128,64]{0,1:T(8,128)(2,1)} %get-tuple-element.57) | copy-start | bytes 49156
  186.5 4.1 %copy-start.2 = (bf16[1,128,16,128]{3,1,2,0:T(8,128)(2,1)S(1)}, bf16[1,128,16,128]{3,1,2,0:T(8,128)(2,1)}, u32[]{:S(2)}) copy-start(bf16[1,128,16,128]{3,1,2,0:T(8,128)(2,1)} %get-tuple-element.43) | copy-start | bytes 1572868
  186.5 6.3 %collective-permute-start.7 = (f32[128,64,16]{0,2,1:T(8,128)}, f32[128,64,16]{0,2,1:T(8,128)}, u32[]{:S(2)}, u32[]{:S(2)}) collective-permute-start(f32[128,64,16]{0,2,1:T(8,128)} %copy.217), channel_id=1, source_target_pairs={{0,128},{128,0},{1,129},{129,1},{2,130},{130,2},{3,131},{131,3},{4... | collective-permute-start | bytes 1572872 | tf_op jit(solution)/shard_map/ppermute | solution.py:294
  190.1 24.6 %collective-permute-start.3 = (bf16[4,512,256]{2,1,0:T(8,128)(2,1)}, bf16[4,512,256]{2,1,0:T(8,128)(2,1)}, u32[]{:S(2)}, u32[]{:S(2)}) collective-permute-start(bf16[4,512,256]{2,1,0:T(8,128)(2,1)} %get-tuple-element.13), channel_id=1, source_target_pairs={{0,128},{128,0},{1,129},{129,1},{2,130},{130,2},{3,131},{131,3},{4... | collective-permute-start | bytes 3145736 | tf_op jit(solution)/shard_map/ppermute | solution.py:294
  192.8 1.7 copy-start.1
  194.5 0.6 copy-start.23
  194.7 1.2 copy-start.11
  195.4 14.0 %copy-start.3 = (f32[8,8,4,4,128]{4,0,3,2,1:T(8,128)S(1)}, f32[8,8,4,4,128]{4,0,3,2,1:T(8,128)}, u32[]{:S(2)}) copy-start(f32[8,8,4,4,128]{4,0,3,2,1:T(8,128)} %copy.194) | copy-start | bytes 1572868
  210.4 4.3 %copy-start.4 = (bf16[4,512,256]{2,1,0:T(8,128)(2,1)S(1)}, bf16[4,512,256]{2,1,0:T(8,128)(2,1)}, u32[]{:S(2)}) copy-start(bf16[4,512,256]{2,1,0:T(8,128)(2,1)} %get-tuple-element.13) | copy-start | bytes 3145732
  210.4 2.9 %collective-permute-start.10 = (bf16[8,128,64]{2,0,1:T(8,128)(2,1)S(1)}, bf16[8,128,64]{2,0,1:T(8,128)(2,1)S(1)}, u32[]{:S(2)}, u32[]{:S(2)}) collective-permute-start(bf16[8,128,64]{2,0,1:T(8,128)(2,1)S(1)} %constant_dynamic-slice_fusion), channel_id=1, source_target_pairs={{0,128},{128,0},{1,129},{129,1},{2,130},{130,2},{3,131},{131,3},{4... | collective-permute-start | bytes 393224 | tf_op jit(solution)/shard_map/ppermute | solution.py:294

commit v3 on v2

--- a/solution.py
+++ b/solution.py
@@ -25,87 +25,6 @@
 
 def dot(a, b, dims):
     return lax.dot_general(a, b, dims, preferred_element_type=jnp.float32)
-
-
-def column_kernel(
-    heads, x_ref, mrow_ref, mcol_ref, gain_ref, w_ref, wo_ref, gain2_ref, wp_ref, mixed_ref, left_ref, right_ref,
-    qkv_ref, gate_ref, gated_ref,
-):
-    width = x_ref.shape[-1]
-    depth = mrow_ref.shape[-1]
-    feats = wo_ref.shape[0]
-    hd = feats // heads
-    x = x_ref[:, 0].reshape(depth, width).astype(jnp.float32)
-    n = standardize_features(x, gain_ref[...]).astype(jnp.bfloat16)
-    proj = dot(w_ref[...], n, NT)
-    for i in range(3):
-        qkv_ref[i] = proj[i * feats : (i + 1) * feats].astype(jnp.bfloat16).reshape(heads, hd, depth)
-    gate_ref[...] = sigmoid(proj[3 * feats :]).reshape(heads, hd, depth)
-    live = mcol_ref[0] > 0.5
-    inv_root = 1.0 / hd**0.5
-
-    def one_head(h):
-        scores = dot(qkv_ref[1, h], qkv_ref[0, h], TN) * inv_root
-        scores = jnp.where(live, scores, -1000000000.0)
-        e = jnp.exp(scores - jnp.max(scores, axis=0, keepdims=True))
-        total = jnp.sum(e, axis=0, keepdims=True)
-        att = jnp.dot(qkv_ref[2, h], e.astype(jnp.bfloat16), preferred_element_type=jnp.float32)
-        gated_ref[h] = (att * (1.0 / total) * gate_ref[h]).astype(jnp.bfloat16)
-
-    unroll = 4
-
-    @pl.loop(0, heads // unroll)
-    def _(step):
-        for u in range(unroll):
-            one_head(step * unroll + u)
-
-    gated = gated_ref[...].reshape(feats, depth)
-    mixed = (x + dot(gated, wo_ref[...], TN)).astype(jnp.bfloat16)
-    mixed_ref[0] = mixed
-    n2 = standardize_features(mixed.astype(jnp.float32), gain2_ref[...]).astype(jnp.bfloat16)
-    panel = (dot(wp_ref[...], n2, NT) * mrow_ref[0]).astype(jnp.bfloat16)
-    chans = left_ref.shape[1]
-    left_ref[0] = panel[:chans]
-    right_ref[0] = panel[chans:]
-
-
-def column_stage(xs, mask_rows, gain, w_t, wo, gain2, wp_t, heads):
-    groups, res, s_loc, width = xs.shape
-    depth = groups * s_loc
-    chans = wp_t.shape[0] // 2
-    whole = lambda a: pl.BlockSpec(a.shape, lambda i: (0,) * a.ndim)
-    mrow = mask_rows[:, None, :]
-    mcol = mask_rows[:, :, None]
-    return pl.pallas_call(
-        functools.partial(column_kernel, heads),
-        grid=(res,),
-        in_specs=[
-            pl.BlockSpec((groups, 1, s_loc, width), lambda i: (0, i, 0, 0)),
-            pl.BlockSpec((1, 1, depth), lambda i: (i, 0, 0)),
-            pl.BlockSpec((1, depth, 1), lambda i: (i, 0, 0)),
-            whole(gain),
-            whole(w_t),
-            whole(wo),
-            whole(gain2),
-            whole(wp_t),
-        ],
-        out_specs=[
-            pl.BlockSpec((1, depth, width), lambda i: (i, 0, 0)),
-            pl.BlockSpec((1, chans, depth), lambda i: (i, 0, 0)),
-            pl.BlockSpec((1, chans, depth), lambda i: (i, 0, 0)),
-        ],
-        out_shape=[
-            jax.ShapeDtypeStruct((res, depth, width), jnp.bfloat16),
-            jax.ShapeDtypeStruct((res, chans, depth), jnp.bfloat16),
-            jax.ShapeDtypeStruct((res, chans, depth), jnp.bfloat16),
-        ],
-        scratch_shapes=[
-            pltpu.VMEM((3, heads, wo.shape[0] // heads, depth), jnp.bfloat16),
-            pltpu.VMEM((heads, wo.shape[0] // heads, depth), jnp.float32),
-            pltpu.VMEM((heads, wo.shape[0] // heads, depth), jnp.bfloat16),
-        ],
-        name="column_attention",
-    )(xs, mrow, mcol, gain, w_t, wo, gain2, wp_t)
 
 
 def remote(src, dst, send_sem, recv_sem, where):
@@ -261,6 +180,161 @@
         compiler_params=pltpu.CompilerParams(collective_id=ident, has_side_effects=True),
         name=name,
     )(left, right)
+
+
+def column_kernel(
+    heads, number, send_ref, msend_ref, gain_ref, gain2_ref, w_ref, wo_ref, ws_ref, wt_ref, *refs
+):
+    extras, (mixed_ref, left_ref, right_ref), both_refs = refs[:number], refs[number : number + 3], refs[number + 3 : 2 * number + 3]
+    (
+        x_ref, m_ref, w2_ref, wo2_ref, ws2_ref, qkv_ref, gate_ref, gated_ref,
+        send_sem, recv_sem, msend_sem, mrecv_sem, keep_sem, tsend_sem, trecv_sem, tkeep_sem,
+    ) = refs[2 * number + 3 :]
+    res, count, s_loc, width = send_ref.shape
+    depth = count * s_loc
+    feats = wo2_ref.shape[0] * wo2_ref.shape[1]
+    hd = feats // heads
+    part = feats // 2
+    me = lax.axis_index("dap")
+    core = lax.axis_index("branch")
+    twin = {"branch": 1 - core}
+    barrier = pltpu.get_barrier_semaphore()
+
+    def hello(d, carry):
+        pl.semaphore_signal(
+            barrier, inc=1, device_id={"dap": lax.rem(me + d, count)}, device_id_type=pl.DeviceIdType.MESH
+        )
+        return carry
+
+    lax.fori_loop(1, count, hello, 0)
+    pl.semaphore_signal(barrier, inc=1, device_id=twin, device_id_type=pl.DeviceIdType.MESH)
+    pl.semaphore_wait(barrier, count)
+
+    def give_mask(d, carry):
+        peer = lax.rem(me + d, count)
+        remote(msend_ref.at[peer], m_ref.at[me], msend_sem.at[0], mrecv_sem.at[0], {"dap": peer}).start()
+        return carry
+
+    lax.fori_loop(1, count, give_mask, 0)
+    pairs = [(w_ref, w2_ref), (wo_ref, wo2_ref), (ws_ref, ws2_ref)] + list(zip(extras, both_refs))
+    swaps = [remote(a, o.at[core], tsend_sem.at[i], trecv_sem.at[i], twin) for i, (a, o) in enumerate(pairs)]
+    for copy in swaps:
+        copy.start()
+    for r in range(res):
+
+        def give(d, carry):
+            peer = lax.rem(me + d, count)
+            remote(send_ref.at[r, peer], x_ref.at[r, me], send_sem.at[r], recv_sem.at[r], {"dap": peer}).start()
+            return carry
+
+        lax.fori_loop(1, count, give, 0)
+    keeps = [pltpu.make_async_copy(a, o.at[core], tkeep_sem.at[i]) for i, (a, o) in enumerate(pairs)]
+    keeps += [pltpu.make_async_copy(send_ref.at[r, me], x_ref.at[r, me], keep_sem.at[r]) for r in range(res)]
+    keeps.append(pltpu.make_async_copy(msend_ref.at[me], m_ref.at[me], keep_sem.at[res]))
+    for copy in keeps:
+        copy.start()
+    for copy in keeps:
+        copy.wait()
+    for i, (a, o) in enumerate(pairs):
+        remote(a, o.at[1 - core], tsend_sem.at[i], trecv_sem.at[i], twin).wait_recv()
+    rest = pl.ds(0, count - 1)
+    masks = remote(msend_ref.at[rest], m_ref.at[rest], msend_sem.at[0], mrecv_sem.at[0], twin)
+    masks.wait_recv()
+
+    m = m_ref[...].reshape(depth, 128)
+    rows = lax.broadcasted_iota(jnp.int32, (8, 128), 0)
+    lanes = lax.broadcasted_iota(jnp.int32, (8, 128), 1)
+    tail = dot((rows == lanes).astype(jnp.bfloat16), m, NT).astype(jnp.bfloat16)
+    chans = wt_ref.shape[0]
+    left_ref[res * chans :] = tail
+    right_ref[res * chans :] = tail
+    inv_root = 1.0 / hd**0.5
+
+    @pl.loop(0, res)
+    def _(r):
+        remote(send_ref.at[r, rest], x_ref.at[r, rest], send_sem.at[r], recv_sem.at[r], twin).wait_recv()
+        x = x_ref[r].reshape(depth, width).astype(jnp.float32)
+        n = standardize_features(x, gain_ref[...]).astype(jnp.bfloat16)
+        for c in range(2):
+            proj = dot(w2_ref[c], n, NT)
+            for i in range(3):
+                qkv_ref[i, c * (heads // 2) : (c + 1) * (heads // 2)] = (
+                    proj[i * part : (i + 1) * part].astype(jnp.bfloat16).reshape(heads // 2, hd, depth)
+                )
+            gate_ref[c * (heads // 2) : (c + 1) * (heads // 2)] = sigmoid(proj[3 * part :]).reshape(heads // 2, hd, depth)
+        lane = lax.broadcasted_iota(jnp.int32, (depth, 128), 1)
+        mcol = jnp.sum(jnp.where(lane == r, m_ref[...].reshape(depth, 128).astype(jnp.float32), 0.0), axis=1, keepdims=True)
+        live = mcol > 0.5
+
+        def one_head(h):
+            scores = dot(qkv_ref[1, h], qkv_ref[0, h], TN) * inv_root
+            scores = jnp.where(live, scores, -1000000000.0)
+            e = jnp.exp(scores - jnp.max(scores, axis=0, keepdims=True))
+            total = jnp.sum(e, axis=0, keepdims=True)
+            att = jnp.dot(qkv_ref[2, h], e.astype(jnp.bfloat16), preferred_element_type=jnp.float32)
+            gated_ref[h] = (att * (1.0 / total) * gate_ref[h]).astype(jnp.bfloat16)
+
+        unroll = 4
+
+        @pl.loop(0, heads // unroll)
+        def _(step):
+            for u in range(unroll):
+                one_head(step * unroll + u)
+
+        gated = gated_ref[...].reshape(feats, depth)
+        mixed = (x + dot(gated, wo2_ref[...].reshape(feats, width), TN)).astype(jnp.bfloat16)
+        mixed_ref[r] = mixed
+        n2 = standardize_features(mixed.astype(jnp.float32), gain2_ref[...]).astype(jnp.bfloat16)
+        mrow = dot((lanes == r).astype(jnp.bfloat16), m_ref[...].reshape(depth, 128), NT)[:1]
+        where = pl.ds(pl.multiple_of(r * chans, chans), chans)
+        left_ref[where] = (dot(ws2_ref[...].reshape(chans, width), n2, NT) * mrow).astype(jnp.bfloat16)
+        right_ref[where] = (dot(wt_ref[...], n2, NT) * mrow).astype(jnp.bfloat16)
+
+    for copy in swaps:
+        copy.wait_send()
+    masks.wait_send()
+    for r in range(res):
+        remote(send_ref.at[r, rest], x_ref.at[r, rest], send_sem.at[r], recv_sem.at[r], twin).wait_send()
+
+
+def column_stage(send, msend, gain, gain2, w_t, wo, ws_t, wt_t, extras, heads):
+    res, groups, s_loc, width = send.shape
+    depth = groups * s_loc
+    chans = wt_t.shape[0]
+    number = len(extras)
+    feats = 2 * wo.shape[0]
+    hd = feats // heads
+    vmem = pl.BlockSpec(memory_space=pltpu.VMEM)
+    hbm = pl.BlockSpec(memory_space=pl.ANY)
+    bf16 = jnp.bfloat16
+    panel = jax.ShapeDtypeStruct((res * chans + 8, depth), bf16)
+    return pl.pallas_call(
+        functools.partial(column_kernel, heads, number),
+        in_specs=[hbm, hbm] + [vmem] * 6 + [hbm] * number,
+        out_specs=[vmem] * 3 + [hbm] * number,
+        out_shape=[jax.ShapeDtypeStruct((res, depth, width), bf16), panel, panel]
+        + [jax.ShapeDtypeStruct((2,) + a.shape, a.dtype) for a in extras],
+        scratch_shapes=[
+            pltpu.VMEM(send.shape, bf16),
+            pltpu.VMEM(msend.shape, bf16),
+            pltpu.VMEM((2,) + w_t.shape, bf16),
+            pltpu.VMEM((2,) + wo.shape, bf16),
+            pltpu.VMEM((2,) + ws_t.shape, bf16),
+            pltpu.VMEM((3, heads, hd, depth), bf16),
+            pltpu.VMEM((heads, hd, depth), jnp.float32),
+            pltpu.VMEM((heads, hd, depth), bf16),
+            pltpu.SemaphoreType.DMA((res,)),
+            pltpu.SemaphoreType.DMA((res,)),
+            pltpu.SemaphoreType.DMA((1,)),
+            pltpu.SemaphoreType.DMA((1,)),
+            pltpu.SemaphoreType.DMA((res + 1,)),
+            pltpu.SemaphoreType.DMA((3 + number,)),
+            pltpu.SemaphoreType.DMA((3 + number,)),
+            pltpu.SemaphoreType.DMA((3 + number,)),
+        ],
+        compiler_params=pltpu.CompilerParams(collective_id=1, has_side_effects=True),
+        name="column_attention",
+    )(send, msend, gain, gain2, w_t, wo, ws_t, wt_t, *extras)
 
 
 def body(
@@ -306,51 +380,47 @@
 
     active = residue_mask.astype(f32)
 
-    fourfold = both(fourfold_projection_matrix, 2)
-    heads, hd = fourfold.shape[2:]
-    feats = heads * hd
-    w_t = fourfold.reshape(width, 4 * feats).T
-    wo = both(mixing_projection_matrix.reshape(-1, width), 0)
-    source = both(product_source_matrix, 1)
-    chans = source.shape[1]
-    wp_t = jnp.concatenate([source, product_target_matrix], axis=1).T
-    outer_w = both(outer_output_weight, 0).reshape(chans * chans, pair_width)
-    tri_in = both(triangle_input_weight, 2)
-    hidden = tri_in.shape[2]
-    tri_in = tri_in.reshape(pair_width, 4 * hidden)
-    tri_gate = both(triangle_gate_weight, 1)
-    hidden_gain = both(hidden_norm_scale, 0)
-    tri_out = both(triangle_output_weight, 0)
+    heads, hd = 2 * fourfold_projection_matrix.shape[2], fourfold_projection_matrix.shape[3]
+    w_t = fourfold_projection_matrix.reshape(width, -1).T
+    wo = mixing_projection_matrix.reshape(-1, width)
+    chans = product_target_matrix.shape[1]
+    hidden = 2 * triangle_input_weight.shape[2]
+    extras = [
+        outer_output_weight.reshape(-1, pair_width),
+        triangle_input_weight.transpose(1, 2, 0),
+        triangle_gate_weight.T,
+        triangle_output_weight,
+        jnp.broadcast_to(hidden_norm_scale[None], (8, hidden // 2)),
+    ]
 
     ny = 4 if groups % 16 == 0 else 2
     nz = groups // ny
     row = lambda i: i - lax.rem(i, nz)
     row_peer = lambda i, d: {"dap": row(i) + lax.rem(lax.rem(i, nz) + d, nz)}
     row_slot = lambda i: lax.rem(i, nz)
-    all_peer = lambda i, d: {"dap": lax.rem(i + d, groups)}
-
-    send = pick(homolog_features, 1, b).reshape(s_loc, groups, half, width).transpose(1, 2, 0, 3)
-    own_mask = pick(alignment_mask.astype(bf16), 1, b).reshape(s_loc, groups, half).transpose(1, 2, 0)
-    own_mask = jnp.pad(own_mask, ((0, 0), (0, 8 - half), (0, 128 - s_loc)))
-    xs, mask_in = scatter([send, own_mask], groups, all_peer, lambda i: i, 1, "feature_exchange")
+
+    send = pick(homolog_features, 1, b).reshape(s_loc, groups, half, width).transpose(2, 1, 0, 3)
+    own_mask = pick((alignment_mask * residue_mask[None, :]).astype(bf16), 1, b)
+    own_mask = own_mask.reshape(s_loc, groups, half).transpose(1, 0, 2)
+    own_mask = jnp.pad(own_mask, ((0, 0), (0, 0), (0, 128 - half)))
     depth = groups * s_loc
-    mask_in = mask_in[:, :half, :s_loc].transpose(1, 0, 2).reshape(half, depth).astype(f32)
-    own_active = lax.dynamic_slice_in_dim(active, me * res + b * half, half, 0)
-    own_t = mask_in * own_active[:, None]
-
-    mixed, left, right = column_stage(
-        xs,
-        own_t,
+    mixed, left, right, outer_w, tri_in, tri_gate, tri_out, hidden_gain = column_stage(
+        send,
+        own_mask,
         vertical_gain_vector[None],
+        product_gain_vector[None],
         w_t,
         wo,
-        product_gain_vector[None],
-        wp_t,
+        product_source_matrix.T,
+        product_target_matrix.T,
+        extras,
         heads,
     )
-    tail = jnp.pad(own_t.astype(bf16), ((0, 8 - half), (0, 0)))
-    left = jnp.concatenate([left.reshape(half * chans, depth), tail], axis=0)
-    right = jnp.concatenate([right.reshape(half * chans, depth), tail], axis=0)
+    outer_w = outer_w.reshape(chans * chans, pair_width)
+    tri_in = tri_in.transpose(1, 0, 2, 3).reshape(4 * hidden, pair_width).T
+    tri_gate = tri_gate.reshape(pair_width, pair_width).T
+    tri_out = tri_out.reshape(hidden, pair_width)
+    hidden_gain = hidden_gain[:, 0].reshape(hidden)
     left, right = gather_blocks(left, right, ny, nz, True, 2, "panel_gather")
     homolog_mixed = both(mixed, 0).transpose(1, 0, 2)
 

time: 220 us -> 203 us (0.923)
  Pallas kernels: 135 us -> 125 us
  local copies, waits for them, and re-layouts: 37 us -> 46.9 us
  other arithmetic: 18.4 us -> 10.2 us
  starting transfers between devices: 11.2 us -> 5.22 us
    pallas_call x3 -> x2, Pallas kernels: 58.8 us -> 24.3 us  [scatter(): pl.pallas_call(functools.partial(scatter_kernel, count, number, peer_of,...]
    pallas_call x1, Pallas kernels: 25.7 us -> 47.6 us  [column_stage(): pl.pallas_call(functools.partial(column_kernel, heads, number), in_specs=...]
    transpose x1 -> x2, local copies, waits for them, and re-layouts: 0.02 us -> 11.5 us  [the longest x1 11.5 us: body(): outer.reshape(rows_i, chans, cols_j, chans).transpose(0, 2, 1, 3)]
    ppermute x11 -> x3, starting transfers between devices: 11.2 us -> 5.22 us  [swap(): return lax.ppermute(a, 'branch', SWAP)]
    concatenate x4 -> x0, other arithmetic: 3.82 us -> none  [the longest x3 2.13 us: both(): jnp.concatenate([jnp.where(first, own, other), jnp.where(first, other, ow...]
    select_n x9 -> x1, other arithmetic: 4.3 us -> 1.36 us  [both(): jnp.where(first, own, other)]
    pallas_call x2, Pallas kernels: 50.4 us -> 52.8 us  [gather_blocks(): pl.pallas_call(functools.partial(block_kernel, ny, nz, share), in_specs=[...]
    unnamed x60 -> x40, local copies, waits for them, and re-layouts: 8.14 us -> 6.6 us
  transfers between devices with their start and end apart: 11 -> 3, of which waited for: 2 -> 1; matrix products, arithmetic and copies ran while one was open for 12% -> 29% of each run, Pallas kernels for 21% -> 38%
where the time goes in v3:
time: 203 us; the launch traced here: 202 us
  Pallas kernels  125 us (62%)
  local copies, waits for them, and re-layouts  46.9 us (23%)
  matrix products  12.5 us (6%)
  other arithmetic  10.2 us (5%)
  starting transfers between devices  5.22 us (3%)
    pallas_call x2, Pallas kernels, gather_blocks(): pl.pallas_call(functools.partial(block_kernel, ny, nz, share), in_specs=[...  52.8 us
    pallas_call x1, Pallas kernels, column_stage(): pl.pallas_call(functools.partial(column_kernel, heads, number), in_specs=...  47.6 us
    pallas_call x2, Pallas kernels, scatter(): pl.pallas_call(functools.partial(scatter_kernel, count, number, peer_of,...  24.3 us
    transpose x1, local copies, waits for them, and re-layouts, body(): outer.reshape(rows_i, chans, cols_j, chans).transpose(0, 2, 1, 3)  11.5 us
    reshape x1, local copies, waits for them, and re-layouts, body(): outer.reshape(rows_i, chans, cols_j, chans).transpose(0, 2, 1, 3)  6.98 us
    unnamed x40, local copies, waits for them, and re-layouts  6.6 us
    ppermute x3, starting transfers between devices, swap(): return lax.ppermute(a, 'branch', SWAP)  5.22 us
  transfers between devices with their start and end apart: 3, of which 1 were waited for; matrix products, arithmetic and copies ran while one was open for 29% of the time, Pallas kernels for 38%

profile of v3, /device:TPU:1, one launch (start us, length us, event | category | flops | bytes accessed | tf_op | source)
XLA Modules:
  0.0 201.8 jit_solution(6133612517532612190)
XLA Ops:
  0.6 0.7 multiply_convert_fusion.1
  1.8 2.5 %reshape.285 = bf16[16,32,2,4,256]{4,3,2,1,0:T(4,128)(2,1)S(1)} reshape(bf16[16,256,256]{2,1,0:T(8,128)(2,1)} %param.16) | data formatting | bytes 4194304 | tf_op jit(solution)/shard_map/reshape | solution.py:377
  4.4 0.4 constant_dynamic-slice_fusion.5
  4.8 1.6 copy.209
  6.4 0.7 pad.4.msend_ref
  7.0 0.6 broadcast_in_dim.8.refs_4_
  7.6 47.6 %column_attention.1 = (bf16[4,512,256]{2,1,0:T(8,128)(2,1)}, bf16[136,512]{1,0:T(8,128)(2,1)}, bf16[136,512]{1,0:T(8,128)(2,1)}, bf16[2,512,128]{2,1,0:T(8,128)(...) custom-call(bf16[4,32,16,256]{3,2,1,0:T(8,128)(2,1)} %bitcast.147, ...), custom_call_target="tpu_custom_call" | custom-call | tf_op jit(solution)/shard_map/column_attention/pallas_call | solution.py:311
  55.3 1.9 collective-permute-start
  57.2 25.1 %panel_gather.1 = (bf16[2,8,136,512]{3,2,1,0:T(8,128)(2,1)}, bf16[4,136,512]{2,1,0:T(8,128)(2,1)}) custom-call(bf16[136,512]{1,0:T(8,128)(2,1)} %get-tuple-element.15.l_ref, bf16[136,512]{1,0:T(8,128)(2,1)} %get-tuple-element.16.r_ref), custom_call_target="tpu_custom_call" | custom-call | tf_op jit(solution)/shard_map/panel_gather/pallas_call | solution.py:171
  82.3 0.8 slice.30
  83.1 1.1 slice.28
  84.2 0.9 slice.29
  85.1 3.2 %slice.27 = bf16[2,8,128,512]{3,2,1,0:T(8,128)(2,1)} slice(bf16[2,8,136,512]{3,2,1,0:T(8,128)(2,1)} %get-tuple-element.17), slice={[0:2], [0:8], [0:128], [0:512]} | slice | bytes 4194304 | tf_op jit(solution)/shard_map/slice | solution.py:430
  88.9 0.3 copy.132
  89.3 3.0 %convolution_convert_fusion = bf16[2048,512]{1,0:T(8,128)(2,1)S(1)} fusion(bf16[2048,512]{1,0:T(8,128)(2,1)} %bitcast.149, bf16[512,512]{1,0:T(8,128)(2,1)S(1)} %bitcast.164), kind=kOutput, calls=%fused_computation | convolution fusion | flops 1074790400 | bytes 4718592 | tf_op jit(solution)/shard_map/dot_general | solution.py:27
  92.3 7.0 %reshape.293 = bf16[64,32,16,32]{3,2,1,0:T(8,128)(2,1)} reshape(bf16[2048,512]{1,0:T(8,128)(2,1)S(1)} %convolution_convert_fusion) | data formatting | bytes 4194304 | tf_op jit(solution)/shard_map/reshape | solution.py:432
  99.3 11.5 %copy.134 = bf16[64,16,32,32]{0,3,2,1:T(8,128)(2,1)} copy(bf16[64,16,32,32]{3,1,2,0:T(8,128)(2,1)} %bitcast.145) | data formatting | bytes 4194304 | tf_op jit(solution)/shard_map/transpose | solution.py:432
  110.9 3.5 %fusion.9 = bf16[64,16,128]{2,0,1:T(8,128)(2,1)S(1)} fusion(bf16[64,16,1024]{0,2,1:T(8,128)(2,1)} %bitcast.146, bf16[1024,128,1]{1,0,2:T(8,128)(2,1)S(1)} %bitcast.181, f32[64,16]{0,1:T(8,128)S(1)} %convolution_maximum_fusion), kind=kOutput, calls=%fused_computation.14 | convolution fusion | flops 268697600 | bytes 2625536 | tf_op jit(solution)/shard_map/dot_general | solution.py:433
  114.5 0.9 copy.136
  115.3 11.0 %update_exchange.1 = bf16[8,8,16,128]{3,2,1,0:T(8,128)(2,1)} custom-call(bf16[8,8,16,128]{3,2,1,0:T(8,128)(2,1)} %bitcast.161), custom_call_target="tpu_custom_call" | custom-call | tf_op jit(solution)/shard_map/update_exchange/pallas_call | solution.py:76
  126.3 1.8 convert_bitcast_fusion.2
  128.5 0.4 fusion.12
  129.4 0.4 fusion.30
  131.1 1.1 fusion.26
  132.2 27.7 %triangle_gather.1 = (bf16[8,128,8,128]{3,2,1,0:T(8,128)(2,1)}, bf16[4,128,8,128]{3,2,1,0:T(8,128)(2,1)}) custom-call(bf16[128,8,128]{2,1,0:T(8,128)(2,1)} %get-tuple-element.53.l_ref, bf16[128,8,128]{2,1,0:T(8,128)(2,1)} %get-tuple-element.52.r_ref), custom_call_target="tpu_custom_call" | custom-call | tf_op jit(solution)/shard_map/triangle_gather/pallas_call | solution.py:171
  159.9 1.6 copy.151
  161.6 0.9 constant_dynamic-slice_fusion.1
  162.5 1.2 fusion
  163.7 1.4 copy.154
  165.1 2.6 %collective-permute-start.1 = (f32[128,64,16]{0,2,1:T(8,128)}, f32[128,64,16]{0,2,1:T(8,128)}, u32[]{:S(2)}, u32[]{:S(2)}) collective-permute-start(f32[128,64,16]{0,2,1:T(8,128)} %copy.154), channel_id=1, source_target_pairs={{0,128},{128,0},{1,129},{129,1},{2,130},{130,2},{3,131},{131,3},{4... | collective-permute-start | bytes 1572872 | tf_op jit(solution)/shard_map/ppermute | solution.py:368
  167.7 1.0 convert_bitcast_fusion
  168.7 0.8 copy.140
  169.5 0.8 copy.133
  170.3 0.7 slice_reduce_fusion
  171.1 0.8 copy.137
  172.0 1.1 fusion.8
  173.1 2.2 %fusion.2 = f32[128,64,16]{1,2,0:T(8,128)S(1)} fusion(bf16[1,128,16,128]{3,1,2,0:T(8,128)(2,1)} %get-tuple-element.47, bf16[8,128,8,128]{3,2,1,0:T(8,128)(2,1)S(1)} %copy-done), kind=kOutput, calls=%fused_computation.4 | convolution fusion | flops 33554432 | bytes 3145728 | tf_op jit(solution)/shard_map/cik,cjk->cij/dot_general | solution.py:468
  175.3 1.6 copy.155
  177.6 0.6 copy.156
  178.2 0.9 convolution_convert_fusion.1
  179.1 13.3 %triangle_exchange.1 = bf16[8,8,16,128]{3,2,1,0:T(8,128)(2,1)} custom-call(bf16[8,8,16,128]{3,2,1,0:T(8,128)(2,1)} %bitcast.160), custom_call_target="tpu_custom_call" | custom-call | tf_op jit(solution)/shard_map/triangle_exchange/pallas_call | solution.py:76
  192.4 1.0 convert_bitcast_fusion.1
  193.4 0.9 fusion.21
  194.5 0.7 collective-permute-start.2
  195.1 1.2 collective-permute-done.2
  196.7 1.0 copy.163
  197.7 1.4 broadcast_select_fusion.1
  199.3 2.5 %copy.162 = bf16[512,8,256]{2,1,0:T(8,128)(2,1)} copy(bf16[512,8,256]{2,0,1:T(8,128)(2,1)S(1)} %maximum_bitcast_fusion) | data formatting | bytes 4194304
  (71 shorter events, 4.7 us)
Async XLA Ops:
  4.4 2.7 %copy-start.12 = (f32[64]{0:T(128)S(1)}, f32[64]{0:T(128)}, u32[]{:S(2)}) copy-start(f32[64]{0:T(128)} %param.30) | copy-start | bytes 772
  4.8 52.4 %copy-start.11 = (s32[256]{0:T(256)S(1)}, s32[256]{0:T(256)}, u32[]{:S(2)}) copy-start(s32[256]{0:T(256)} %param.18) | copy-start | bytes 3076
  55.3 142.5 %collective-permute-start = (bf16[4,512,256]{2,1,0:T(8,128)(2,1)}, bf16[4,512,256]{2,1,0:T(8,128)(2,1)}, u32[]{:S(2)}, u32[]{:S(2)}) collective-permute-start(bf16[4,512,256]{2,1,0:T(8,128)(2,1)} %get-tuple-element.14), channel_id=1, source_target_pairs={{0,128},{128,0},{1,129},{129,1},{2,130},{130,2},{3,131},{131,3},{4... | collective-permute-start | bytes 3145736 | tf_op jit(solution)/shard_map/ppermute | solution.py:368
  85.1 3.7 %copy-start.6 = (bf16[8,256,128]{2,1,0:T(8,128)(2,1)S(1)}, bf16[8,256,128]{2,1,0:T(8,128)(2,1)}, u32[]{:S(2)}) copy-start(bf16[8,256,128]{2,1,0:T(8,128)(2,1)} %param.19) | copy-start | bytes 1572868
  85.1 4.1 %copy-start.9 = (bf16[2,4,64,128]{3,2,1,0:T(8,128)(2,1)S(1)}, bf16[2,4,64,128]{3,2,1,0:T(8,128)(2,1)}, u32[]{:S(2)}) copy-start(bf16[2,4,64,128]{3,2,1,0:T(8,128)(2,1)} %get-tuple-element.21) | copy-start | bytes 393220
  89.2 39.0 %copy-start.2 = (bf16[8,256,128]{2,0,1:T(8,128)(2,1)}, bf16[8,256,128]{2,0,1:T(8,128)(2,1)S(1)}, u32[]{:S(2)}) copy-start(bf16[8,256,128]{2,0,1:T(8,128)(2,1)S(1)} %copy.132) | copy-start | bytes 1572868
  99.3 11.7 %copy-start.14 = (bf16[2,512,128]{2,1,0:T(8,128)(2,1)S(1)}, bf16[2,512,128]{2,1,0:T(8,128)(2,1)}, u32[]{:S(2)}) copy-start(bf16[2,512,128]{2,1,0:T(8,128)(2,1)} %get-tuple-element.19) | copy-start | bytes 786436
  114.4 14.5 %copy-start.13 = (f32[128]{0:T(128)S(1)}, f32[128]{0:T(128)}, u32[]{:S(2)}) copy-start(f32[128]{0:T(128)} %param.27) | copy-start | bytes 1540
  159.9 2.5 %copy-start = (bf16[8,128,8,128]{3,2,1,0:T(8,128)(2,1)S(1)}, bf16[8,128,8,128]{3,2,1,0:T(8,128)(2,1)}, u32[]{:S(2)}) copy-start(bf16[8,128,8,128]{3,2,1,0:T(8,128)(2,1)} %get-tuple-element.22) | copy-start | bytes 6291460
  165.0 6.1 %copy-start.1 = (f32[8,8,16,128]{3,2,0,1:T(8,128)S(1)}, f32[8,8,16,128]{3,2,0,1:T(8,128)}, u32[]{:S(2)}) copy-start(f32[8,8,16,128]{3,2,0,1:T(8,128)} %get-tuple-element.50) | copy-start | bytes 1572868
  165.1 6.9 %copy-start.15 = (bf16[2,64,128]{2,1,0:T(8,128)(2,1)S(1)}, bf16[2,64,128]{2,1,0:T(8,128)(2,1)}, u32[]{:S(2)}) copy-start(bf16[2,64,128]{2,1,0:T(8,128)(2,1)} %get-tuple-element.20) | copy-start | bytes 98308
  165.1 10.2 %collective-permute-start.1 = (f32[128,64,16]{0,2,1:T(8,128)}, f32[128,64,16]{0,2,1:T(8,128)}, u32[]{:S(2)}, u32[]{:S(2)}) collective-permute-start(f32[128,64,16]{0,2,1:T(8,128)} %copy.154), channel_id=1, source_target_pairs={{0,128},{128,0},{1,129},{129,1},{2,130},{130,2},{3,131},{131,3},{4... | collective-permute-start | bytes 1572872 | tf_op jit(solution)/shard_map/ppermute | solution.py:368
  169.5 2.5 %copy-start.8 = (bf16[8,8,4,4,128]{4,3,2,1,0:T(4,128)(2,1)S(1)}, bf16[8,8,4,4,128]{4,3,2,1,0:T(4,128)(2,1)}, u32[]{:S(2)}) copy-start(bf16[8,8,4,4,128]{4,3,2,1,0:T(4,128)(2,1)} %copy.140) | copy-start | bytes 786436
  177.1 1.1 copy-start.10
  177.5 15.9 %copy-start.3 = (f32[8,8,4,4,128]{4,0,3,2,1:T(8,128)S(1)}, f32[8,8,4,4,128]{4,0,3,2,1:T(8,128)}, u32[]{:S(2)}) copy-start(f32[8,8,4,4,128]{4,0,3,2,1:T(8,128)} %copy.133) | copy-start | bytes 1572868
  177.6 15.9 %copy-start.4 = (f32[8,8,16,128]{3,2,1,0:T(8,128)S(1)}, f32[8,8,16,128]{3,2,1,0:T(8,128)}, u32[]{:S(2)}) copy-start(f32[8,8,16,128]{3,2,1,0:T(8,128)} %copy.137) | copy-start | bytes 1572868
  177.6 15.9 %copy-start.7 = (f32[1024,128]{1,0:T(8,128)S(1)}, f32[1024,128]{1,0:T(8,128)}, u32[]{:S(2)}) copy-start(f32[1024,128]{1,0:T(8,128)} %fusion.8) | copy-start | bytes 1572868
  194.5 3.3 %copy-start.5 = (bf16[4,512,256]{2,1,0:T(8,128)(2,1)S(1)}, bf16[4,512,256]{2,1,0:T(8,128)(2,1)}, u32[]{:S(2)}) copy-start(bf16[4,512,256]{2,1,0:T(8,128)(2,1)} %get-tuple-element.14) | copy-start | bytes 3145732
  194.5 1.8 collective-permute-start.2

commit v4 on v3

--- a/solution.py
+++ b/solution.py
@@ -337,6 +337,76 @@
     )(send, msend, gain, gain2, w_t, wo, ws_t, wt_t, *extras)
 
 
+def outer_kernel(nz, left_ref, right_ref, inv_ref, w_ref, out_ref, prod_ref, made_ref, send_sem, recv_sem, local_sem):
+    me = lax.axis_index("dap")
+    z = lax.rem(me, nz)
+    barrier = pltpu.get_barrier_semaphore()
+    peers = [lax.rem(z + d, nz) for d in range(nz)]
+    for d in range(1, nz):
+        pl.semaphore_signal(
+            barrier, inc=1, device_id={"dap": me - z + peers[d]}, device_id_type=pl.DeviceIdType.MESH
+        )
+    ny = right_ref.shape[0]
+    cols, chans = made_ref.shape[1], w_ref.shape[0] // (prod_ref.shape[1] // (2 * inv_ref.shape[0]))
+    rows = inv_ref.shape[0]
+    wide = 2 * rows
+    pairs = prod_ref.shape[1] // wide
+    right = jnp.concatenate([right_ref[y, : (cols // ny) * chans] for y in range(ny)], axis=0)
+    step = min(512, prod_ref.shape[1])
+    for c in range(0, prod_ref.shape[1], step):
+        prod_ref[:, c : c + step] = dot(right, left_ref[c : c + step], NT).astype(jnp.bfloat16)
+    pl.semaphore_wait(barrier, nz - 1)
+    group = 4
+    sends = []
+    for j in range(cols):
+        block = prod_ref[j * chans : (j + 1) * chans]
+        block = jnp.concatenate([block[:, p * wide : (p + 1) * wide] for p in range(pairs)], axis=0)
+        both = dot(block, w_ref[...], TN)
+        width = both.shape[1] // 2
+        total = (both[:rows, :width] + both[rows:, width:]) * inv_ref[:, j : j + 1]
+        made_ref[:, j] = total.reshape(nz, rows // nz, width).astype(jnp.bfloat16)
+        if j % group == group - 1:
+            part = pl.ds(j + 1 - group, group)
+            for d in range(1, nz):
+                copy = remote(
+                    made_ref.at[peers[d], part], out_ref.at[z, part], send_sem.at[d], recv_sem.at[d],
+                    {"dap": me - z + peers[d]},
+                )
+                copy.start()
+    keep = pltpu.make_async_copy(made_ref.at[z], out_ref.at[z], local_sem.at[0])
+    keep.start()
+    for d in range(1, nz):
+        source = lax.rem(z + nz - d, nz)
+        whole = remote(
+            made_ref.at[source], out_ref.at[source], send_sem.at[d], recv_sem.at[d], {"dap": me - z + peers[d]}
+        )
+        whole.wait_recv()
+        whole.wait_send()
+    keep.wait()
+
+
+def outer_stage(left, right, inv, w, nz, chans):
+    rows, cols = inv.shape
+    width = w.shape[1] // 2
+    vmem = pl.BlockSpec(memory_space=pltpu.VMEM)
+    shape = (nz, cols, rows // nz, width)
+    return pl.pallas_call(
+        functools.partial(outer_kernel, nz),
+        in_specs=[vmem] * 4,
+        out_specs=pl.BlockSpec(memory_space=pl.ANY),
+        out_shape=jax.ShapeDtypeStruct(shape, jnp.bfloat16),
+        scratch_shapes=[
+            pltpu.VMEM((cols * chans, left.shape[0]), jnp.bfloat16),
+            pltpu.VMEM(shape, jnp.bfloat16),
+            pltpu.SemaphoreType.DMA((nz,)),
+            pltpu.SemaphoreType.DMA((nz,)),
+            pltpu.SemaphoreType.DMA((1,)),
+        ],
+        compiler_params=pltpu.CompilerParams(collective_id=3, has_side_effects=True),
+        name="outer_product",
+    )(left, right, inv, w)
+
+
 def body(
     homolog_features,
     alignment_mask,
@@ -416,7 +486,8 @@
         extras,
         heads,
     )
-    outer_w = outer_w.reshape(chans * chans, pair_width)
+    outer_w = outer_w.reshape(chans // 2, 2, chans, pair_width).transpose(0, 2, 1, 3)
+    outer_w = outer_w.reshape(chans // 2 * chans, 2 * pair_width)
     tri_in = tri_in.transpose(1, 0, 2, 3).reshape(4 * hidden, pair_width).T
     tri_gate = tri_gate.reshape(pair_width, pair_width).T
     tri_out = tri_out.reshape(hidden, pair_width)
@@ -426,19 +497,14 @@
 
     panel_rows = half * chans
     rows_i, cols_j = 2 * nz * half, ny * half
-    outer = dot(
-        left[:, :, :panel_rows].reshape(rows_i * chans, depth), right[:, :panel_rows].reshape(cols_j * chans, depth), NT
-    ).astype(bf16)
-    outer = outer.reshape(rows_i, chans, cols_j, chans).transpose(0, 2, 1, 3).reshape(rows_i * cols_j, chans * chans)
-    update = jnp.dot(outer, outer_w, preferred_element_type=f32).reshape(rows_i, cols_j, pair_width)
+    left_rows = left[:, :, :panel_rows].reshape(2, nz, half, chans, depth)
+    left_rows = left_rows.transpose(3, 1, 0, 2, 4).reshape(chans * rows_i, depth)
     counts = dot(
-        left[:, :, panel_rows : panel_rows + half].reshape(rows_i, depth),
+        left[:, :, panel_rows : panel_rows + half].transpose(1, 0, 2, 3).reshape(rows_i, depth),
         right[:, panel_rows : panel_rows + half].reshape(cols_j, depth),
         NT,
     )
-    update = (update / jnp.maximum(counts, 1.0)[..., None]).astype(bf16)
-    update = update.reshape(2, nz, half, cols_j, pair_width).transpose(1, 0, 2, 3, 4)
-    (update,) = scatter([update.reshape(nz, res, cols_j, pair_width)], nz, row_peer, row_slot, 3, "update_exchange")
+    update = outer_stage(left_rows, right, 1.0 / jnp.maximum(counts, 1.0), outer_w, nz, chans)
 
     def arrange(a):
         a = a.reshape(a.shape[:1] + (ny, nz, 2, half) + a.shape[2:])
@@ -446,7 +512,7 @@
         return jnp.swapaxes(a, 1, 2).reshape((a.shape[0], groups * half) + a.shape[4:])
 
     cols = groups * half
-    update = update.transpose(1, 0, 2, 3).reshape(res, cols, pair_width).astype(f32)
+    update = update.transpose(2, 0, 1, 3).reshape(res, cols, pair_width).astype(f32)
     pair_mid = (arrange(pairwise_state).astype(f32) + update).astype(bf16)
     pair_field = pair_mid.astype(f32)
     pair_normed = standardize_features(pair_field, triangle_norm_scale).astype(bf16).reshape(res * cols, pair_width)

time: 203 us -> 188 us (0.926)
  local copies, waits for them, and re-layouts: 46.9 us -> 35.9 us
  matrix products: 12.5 us -> 7.6 us
  Pallas kernels: 125 us -> 128 us
    pallas_call x0 -> x1, Pallas kernels: none -> 13.2 us  [outer_stage(): pl.pallas_call(functools.partial(outer_kernel, nz), in_specs=[vmem] * 4,...]
    pallas_call x2 -> x1, Pallas kernels: 24.3 us -> 12.9 us  [scatter(): pl.pallas_call(functools.partial(scatter_kernel, count, number, peer_of,...]
    transpose x1 -> x2, local copies, waits for them, and re-layouts: 11.5 us -> 0.95 us  [body(): left[:, :, panel_rows:panel_rows + half].transpose(1, 0, 2, 3)]
    dot_general x1 -> x0, matrix products: 3.5 us -> none  [body(): jnp.dot(outer, outer_w, preferred_element_type=f32)]
    slice x3 -> x1, local copies, waits for them, and re-layouts: 5.16 us -> 1.8 us  [body(): left_rows = left[:, :, :panel_rows].reshape(2, nz, half, chans, depth)]
    convert_element_type x4 -> x0, local copies, waits for them, and re-layouts: 2.51 us -> none  [the longest x1 0.85 us: body(): update.transpose(1, 0, 2, 3).reshape(res, cols, pair_width).astype(f32)]
    dot_general x3 -> x2, matrix products: 4.04 us -> 1.67 us  [dot(): return lax.dot_general(a, b, dims, preferred_element_type=jnp.float32)]
    unnamed x40 -> x38, local copies, waits for them, and re-layouts: 6.6 us -> 7.88 us
  transfers between devices with their start and end apart: 3 -> 3, of which waited for: 1 -> 1; matrix products, arithmetic and copies ran while one was open for 29% -> 6% of each run, Pallas kernels for 38% -> 7%
where the time goes in v4:
time: 188 us; the launch traced here: 187 us
  Pallas kernels  128 us (68%)
  local copies, waits for them, and re-layouts  35.9 us (19%)
  other arithmetic  8.71 us (5%)
  matrix products  7.6 us (4%)
  starting transfers between devices  4.61 us (2%)
    pallas_call x2, Pallas kernels, gather_blocks(): pl.pallas_call(functools.partial(block_kernel, ny, nz, share), in_specs=[...  54.5 us
    pallas_call x1, Pallas kernels, column_stage(): pl.pallas_call(functools.partial(column_kernel, heads, number), in_specs=...  47.6 us
    pallas_call x1, Pallas kernels, outer_stage(): pl.pallas_call(functools.partial(outer_kernel, nz), in_specs=[vmem] * 4,...  13.2 us
    pallas_call x1, Pallas kernels, scatter(): pl.pallas_call(functools.partial(scatter_kernel, count, number, peer_of,...  12.9 us
    unnamed x38, local copies, waits for them, and re-layouts  7.88 us
    ppermute x3, starting transfers between devices, swap(): return lax.ppermute(a, 'branch', SWAP)  4.61 us
    dot_general x2, matrix products, share_of(): jnp.einsum('cik,cjk->cij', tri_left, chosen, preferred_element_type=f32)  4.39 us
    reshape x1, local copies, waits for them, and re-layouts, body(): left_rows.transpose(3, 1, 0, 2, 4).reshape(chans * rows_i, depth)  4.01 us
  transfers between devices with their start and end apart: 3, of which 1 were waited for; matrix products, arithmetic and copies ran while one was open for 6% of the time, Pallas kernels for 7%

profile of v4, /device:TPU:1, one launch (start us, length us, event | category | flops | bytes accessed | tf_op | source)
XLA Modules:
  0.0 187.2 jit_solution(2984967777421973859)
XLA Ops:
  0.7 2.6 %reshape.274 = bf16[16,32,2,4,256]{4,3,2,1,0:T(4,128)(2,1)S(1)} reshape(bf16[16,256,256]{2,1,0:T(8,128)(2,1)} %param.16) | data formatting | bytes 4194304 | tf_op jit(solution)/shard_map/reshape | solution.py:447
  3.3 0.4 constant_dynamic-slice_fusion.6
  3.7 1.6 copy.164
  5.4 0.3 copy.93
  5.7 0.7 pad.4.msend_ref
  6.4 0.6 broadcast_in_dim.8.refs_4_
  7.0 47.6 %column_attention.1 = (bf16[4,512,256]{2,1,0:T(8,128)(2,1)}, bf16[136,512]{1,0:T(8,128)(2,1)}, bf16[136,512]{1,0:T(8,128)(2,1)}, bf16[2,512,128]{2,1,0:T(8,128)(...) custom-call(bf16[4,32,16,256]{3,2,1,0:T(8,128)(2,1)} %bitcast.152, ...), custom_call_target="tpu_custom_call" | custom-call | tf_op jit(solution)/shard_map/column_attention/pallas_call | solution.py:311
  54.6 27.7 %panel_gather.1 = (bf16[2,8,136,512]{3,2,1,0:T(8,128)(2,1)}, bf16[4,136,512]{2,1,0:T(8,128)(2,1)}) custom-call(bf16[136,512]{1,0:T(8,128)(2,1)} %get-tuple-element.15.l_ref, bf16[136,512]{1,0:T(8,128)(2,1)} %get-tuple-element.16.r_ref), custom_call_target="tpu_custom_call" | custom-call | tf_op jit(solution)/shard_map/panel_gather/pallas_call | solution.py:171
  82.4 0.9 slice_bitcast_fusion
  83.3 1.8 slice.24
  85.2 0.8 slice.26
  85.9 2.9 %copy.163 = bf16[2,8,4,32,512]{4,2,0,1,3:T(4,128)(2,1)} copy(bf16[2,8,4,32,512]{4,3,2,1,0:T(8,128)(2,1)S(1)} %bitcast.148) | data formatting | bytes 4194304 | tf_op jit(solution)/shard_map/reshape | solution.py:500
  88.9 4.0 %reshape.281.left_ref = bf16[2048,512]{1,0:T(8,128)(2,1)} reshape(bf16[32,8,2,4,512]{4,3,2,1,0:T(4,128)(2,1)} %bitcast.149) | data formatting | bytes 4194304 | tf_op jit(solution)/shard_map/reshape | solution.py:501
  92.9 0.2 copy.100
  93.1 0.7 copy.165
  93.9 0.8 fusion.9.inv_ref
  94.6 13.2 %outer_product.1 = bf16[8,16,8,128]{3,2,1,0:T(8,128)(2,1)} custom-call(bf16[2048,512]{1,0:T(8,128)(2,1)} %reshape.281.left_ref, bf16[4,136,512]{2,1,0:T(8,128)(2,1)} %get-tuple-element.18.right_ref, f32[64,16]{1,0:T(8,128)} %fusion.9.inv_ref, bf16[512,256]{1,0:T(8,128)(2,1)} %bitcast.156), custom_call_target="tpu_custom_call" | custom-call | tf_op jit(solution)/shard_map/outer_product/pallas_call | solution.py:393
  107.8 1.0 convert_element_type.161
  108.9 0.5 convert_reduce_fusion
  109.4 0.8 fusion.12
  110.2 0.6 fusion.14
  110.9 0.4 fusion.31
  111.3 1.0 fusion.30
  112.5 0.2 copy.127
  113.0 1.3 copy.129
  114.9 1.1 fusion.27
  116.0 26.8 %triangle_gather.1 = (bf16[8,128,8,128]{3,2,1,0:T(8,128)(2,1)}, bf16[4,128,8,128]{3,2,1,0:T(8,128)(2,1)}) custom-call(bf16[128,8,128]{2,1,0:T(8,128)(2,1)} %get-tuple-element.49.l_ref, bf16[128,8,128]{2,1,0:T(8,128)(2,1)} %get-tuple-element.48.r_ref), custom_call_target="tpu_custom_call" | custom-call | tf_op jit(solution)/shard_map/triangle_gather/pallas_call | solution.py:171
  142.8 2.6 %copy.111 = bf16[4,128,2,4,128]{4,1,3,0,2:T(8,128)(2,1)} copy(bf16[4,128,2,4,128]{4,3,2,1,0:T(4,128)(2,1)} %bitcast.159) | data formatting | bytes 2097152 | tf_op jit(solution)/shard_map/reshape | solution.py:530
  145.4 2.1 %constant_dynamic-slice_fusion.1 = (bf16[1,128,16,128]{3,1,2,0:T(8,128)(2,1)S(1)}, bf16[1,128,16,128]{3,1,2,0:T(8,128)(2,1)}) fusion(bf16[2,128,16,128]{3,1,2,0:T(8,128)(2,1)} %bitcast.153, s32[]{:T(128)S(6)} %select_n.76, s32[]{:T(128)S(6)} %select_n.71), kind=kLoop, calls=%fused_computation.61 | loop fusion | bytes 2097160 | tf_op jit(solution)/shard_map/jit(dynamic_index_in_dim)/dynamic_slice | solution.py:533
  147.5 2.2 %fusion = f32[128,64,16]{1,2,0:T(8,128)} fusion(bf16[1,128,16,128]{3,1,2,0:T(8,128)(2,1)S(1)} %get-tuple-element.44, bf16[8,128,8,128]{3,2,1,0:T(8,128)(2,1)S(1)} %copy-done.1), kind=kOutput, calls=%fused_computation.1 | convolution fusion | flops 33554432 | bytes 3145728 | tf_op jit(solution)/shard_map/cik,cjk->cij/dot_general | solution.py:534
  149.7 2.5 %copy.114 = f32[128,64,16]{0,2,1:T(8,128)} copy(f32[128,64,16]{1,2,0:T(8,128)} %fusion) | data formatting | bytes 1048576 | tf_op jit(solution)/shard_map/cik,cjk->cij/dot_general | solution.py:534
  152.2 3.1 %collective-permute-start.1 = (f32[128,64,16]{0,2,1:T(8,128)}, f32[128,64,16]{0,2,1:T(8,128)}, u32[]{:S(2)}, u32[]{:S(2)}) collective-permute-start(f32[128,64,16]{0,2,1:T(8,128)} %copy.114), channel_id=1, source_target_pairs={{0,128},{128,0},{1,129},{129,1},{2,130},{130,2},{3,131},{131,3},{4... | collective-permute-start | bytes 1572872 | tf_op jit(solution)/shard_map/ppermute | solution.py:438
  155.3 0.9 fusion.25
  156.2 0.7 slice_reduce_fusion
  157.0 1.1 fusion.8
  158.1 2.2 %fusion.2 = f32[128,64,16]{1,2,0:T(8,128)} fusion(bf16[1,128,16,128]{3,1,2,0:T(8,128)(2,1)S(1)} %copy-done.3, bf16[8,128,8,128]{3,2,1,0:T(8,128)(2,1)S(1)} %copy-done.1), kind=kOutput, calls=%fused_computation.3 | convolution fusion | flops 33554432 | bytes 3145728 | tf_op jit(solution)/shard_map/cik,cjk->cij/dot_general | solution.py:534
  160.3 1.7 copy.115
  162.7 0.6 copy.116
  163.3 0.9 convolution_convert_fusion
  164.2 12.9 %triangle_exchange.1 = bf16[8,8,16,128]{3,2,1,0:T(8,128)(2,1)} custom-call(bf16[8,8,16,128]{3,2,1,0:T(8,128)(2,1)} %bitcast.162), custom_call_target="tpu_custom_call" | custom-call | tf_op jit(solution)/shard_map/triangle_exchange/pallas_call | solution.py:76
  177.1 1.0 convert_bitcast_fusion
  178.5 1.5 collective-permute-start.2
  180.0 1.2 collective-permute-done.2
  181.4 0.3 copy.118
  181.7 0.3 copy.119
  182.1 1.0 copy.121
  183.2 1.4 broadcast_select_fusion.1
  184.7 2.5 %copy.120 = bf16[512,8,256]{2,1,0:T(8,128)(2,1)} copy(bf16[512,8,256]{2,0,1:T(8,128)(2,1)S(1)} %maximum_bitcast_fusion) | data formatting | bytes 4194304
  (64 shorter events, 3.1 us)
Async XLA Ops:
  0.6 108.2 %copy-start = (bf16[8,256,128]{2,1,0:T(8,128)(2,1)S(1)}, bf16[8,256,128]{2,1,0:T(8,128)(2,1)}, u32[]{:S(2)}) copy-start(bf16[8,256,128]{2,1,0:T(8,128)(2,1)} %param.19) | copy-start | bytes 1572868
  3.3 2.0 %copy-start.10 = (s32[16,256]{1,0:T(8,128)S(1)}, s32[16,256]{1,0:T(8,128)}, u32[]{:S(2)}) copy-start(s32[16,256]{1,0:T(8,128)} %param.17) | copy-start | bytes 49156
  3.3 2.0 %copy-start.11 = (s32[256]{0:T(256)S(1)}, s32[256]{0:T(256)}, u32[]{:S(2)}) copy-start(s32[256]{0:T(256)} %param.18) | copy-start | bytes 3076
  3.3 3.1 %copy-start.12 = (f32[64]{0:T(128)S(1)}, f32[64]{0:T(128)}, u32[]{:S(2)}) copy-start(f32[64]{0:T(128)} %param.30) | copy-start | bytes 772
  88.9 4.0 %copy-start.7 = (bf16[2,512,128]{2,1,0:T(8,128)(2,1)S(1)}, bf16[2,512,128]{2,1,0:T(8,128)(2,1)}, u32[]{:S(2)}) copy-start(bf16[2,512,128]{2,1,0:T(8,128)(2,1)} %get-tuple-element.19) | copy-start | bytes 786436
  107.8 2.4 %copy-start.8 = (bf16[2,4,64,128]{3,2,1,0:T(8,128)(2,1)S(1)}, bf16[2,4,64,128]{3,2,1,0:T(8,128)(2,1)}, u32[]{:S(2)}) copy-start(bf16[2,4,64,128]{3,2,1,0:T(8,128)(2,1)} %get-tuple-element.21) | copy-start | bytes 393220
  107.8 2.4 %copy-start.13 = (f32[128]{0:T(128)S(1)}, f32[128]{0:T(128)}, u32[]{:S(2)}) copy-start(f32[128]{0:T(128)} %param.27) | copy-start | bytes 1540
  142.8 4.7 %copy-start.1 = (bf16[8,128,8,128]{3,2,1,0:T(8,128)(2,1)S(1)}, bf16[8,128,8,128]{3,2,1,0:T(8,128)(2,1)}, u32[]{:S(2)}) copy-start(bf16[8,128,8,128]{3,2,1,0:T(8,128)(2,1)} %get-tuple-element.22) | copy-start | bytes 6291460
  149.7 7.3 %copy-start.14 = (bf16[2,64,128]{2,1,0:T(8,128)(2,1)S(1)}, bf16[2,64,128]{2,1,0:T(8,128)(2,1)}, u32[]{:S(2)}) copy-start(bf16[2,64,128]{2,1,0:T(8,128)(2,1)} %get-tuple-element.20) | copy-start | bytes 98308
  152.2 8.1 %collective-permute-start.1 = (f32[128,64,16]{0,2,1:T(8,128)}, f32[128,64,16]{0,2,1:T(8,128)}, u32[]{:S(2)}, u32[]{:S(2)}) collective-permute-start(f32[128,64,16]{0,2,1:T(8,128)} %copy.114), channel_id=1, source_target_pairs={{0,128},{128,0},{1,129},{129,1},{2,130},{130,2},{3,131},{131,3},{4... | collective-permute-start | bytes 1572872 | tf_op jit(solution)/shard_map/ppermute | solution.py:438
  155.3 27.9 %collective-permute-start = (bf16[4,512,256]{2,1,0:T(8,128)(2,1)}, bf16[4,512,256]{2,1,0:T(8,128)(2,1)}, u32[]{:S(2)}, u32[]{:S(2)}) collective-permute-start(bf16[4,512,256]{2,1,0:T(8,128)(2,1)} %get-tuple-element.14), channel_id=1, source_target_pairs={{0,128},{128,0},{1,129},{129,1},{2,130},{130,2},{3,131},{131,3},{4... | collective-permute-start | bytes 3145736 | tf_op jit(solution)/shard_map/ppermute | solution.py:438
  157.0 1.1 copy-start.3
  160.3 1.7 copy-start.2
  162.2 1.1 copy-start.9
  162.6 15.5 %copy-start.4 = (f32[8,4,8,4,128]{4,3,1,2,0:T(4,128)S(1)}, f32[8,4,8,4,128]{4,3,1,2,0:T(4,128)}, u32[]{:S(2)}) copy-start(f32[8,4,8,4,128]{4,3,1,2,0:T(4,128)} %fusion.25) | copy-start | bytes 1572868
  162.6 15.5 %copy-start.6 = (f32[1024,128]{1,0:T(8,128)S(1)}, f32[1024,128]{1,0:T(8,128)}, u32[]{:S(2)}) copy-start(f32[1024,128]{1,0:T(8,128)} %fusion.8) | copy-start | bytes 1572868
  178.4 4.7 %copy-start.5 = (bf16[4,512,256]{2,1,0:T(8,128)(2,1)S(1)}, bf16[4,512,256]{2,1,0:T(8,128)(2,1)}, u32[]{:S(2)}) copy-start(bf16[4,512,256]{2,1,0:T(8,128)(2,1)} %get-tuple-element.14) | copy-start | bytes 3145732
  178.5 2.7 %collective-permute-start.2 = (bf16[8,128,64]{2,1,0:T(8,128)(2,1)S(1)}, bf16[8,128,64]{2,1,0:T(8,128)(2,1)S(1)}, u32[]{:S(2)}, u32[]{:S(2)}) collective-permute-start(bf16[8,128,64]{2,1,0:T(8,128)(2,1)S(1)} %constant_dynamic-slice_fusion), channel_id=1, source_target_pairs={{0,128},{128,0},{1,129},{129,1},{2,130},{130,2},{3,131},{131,3},{4... | collective-permute-start | bytes 393224 | tf_op jit(solution)/shard_map/ppermute | solution.py:438

commit v5 on v4

--- a/solution.py
+++ b/solution.py
@@ -99,66 +99,79 @@
     column = [{"dap": lax.rem(y + d, ny) * nz + z} for d in range(1, ny)]
     twin = {"branch": 1 - core}
     greet([up, down] + column + ([twin] if share else []))
-    fwd, bwd = nz // 2, nz - 1 - nz // 2
-
-    def slot(which, place):
-        return lg_ref.at[which, place] if share else lg_ref.at[place]
+    long, short = nz // 2, nz - 1 - nz // 2
+    fwd, bwd = (long, short), (short, long)
+    cut = l_ref.shape[0] // 32 * 16
+    spans = (pl.ds(0, cut), pl.ds(cut, l_ref.shape[0] - cut))
+
+    def slot(which, place, q):
+        return lg_ref.at[which, place, spans[q]] if share else lg_ref.at[place, spans[q]]
 
     def at(shift):
         return lax.rem(z + nz + shift, nz)
 
-    def ahead(t):
-        return remote(l_ref if t == 0 else slot(core, at(-t)), slot(core, at(-t)), fsend.at[t], frecv.at[t], up)
-
-    def back(t):
-        return remote(l_ref if t == 0 else slot(core, at(t)), slot(core, at(t)), bsend.at[t], brecv.at[t], down)
-
-    def ahead_in(t):
-        return remote(l_ref, slot(core, at(-1 - t)), fsend.at[t], frecv.at[t], up)
-
-    def back_in(t):
-        return remote(l_ref, slot(core, at(1 + t)), bsend.at[t], brecv.at[t], down)
-
-    def pass_on(i, shift):
-        return remote(l_ref if shift == 0 else slot(core, at(shift)), slot(core, at(shift)), ssend.at[i], srecv.at[i], twin)
-
-    shifts = [0]
-    sends = [ahead(0)] + ([back(0)] if bwd else [])
-    sends += [remote(r_ref, rg_ref.at[y], ysend.at[d], yrecv.at[d], column[d]) for d in range(ny - 1)]
-    if share:
-        sends.append(pass_on(0, 0))
-    for copy in sends:
+    def held(shift, q):
+        return l_ref.at[spans[q]] if shift == 0 else slot(core, at(shift), q)
+
+    def ahead(t, q):
+        return remote(held(-t, q), slot(core, at(-t), q), fsend.at[q, t], frecv.at[q, t], up)
+
+    def back(t, q):
+        return remote(held(t, q), slot(core, at(t), q), bsend.at[q, t], brecv.at[q, t], down)
+
+    def ahead_in(t, q):
+        return remote(held(0, q), slot(core, at(-1 - t), q), fsend.at[q, t], frecv.at[q, t], up)
+
+    def back_in(t, q):
+        return remote(held(0, q), slot(core, at(1 + t), q), bsend.at[q, t], brecv.at[q, t], down)
+
+    def pass_on(i, shift, q):
+        return remote(held(shift, q), slot(core, at(shift), q), ssend.at[q, i], srecv.at[q, i], twin)
+
+    shifts = ([], [])
+    sends = []
+
+    def follow(copy):
         copy.start()
+        sends.append(copy)
+
+    def hand_over(shift, q):
+        if share:
+            shifts[q].append(shift)
+            follow(pass_on(len(shifts[q]) - 1, shift, q))
+
+    for q in range(2):
+        if fwd[q]:
+            follow(ahead(0, q))
+        if bwd[q]:
+            follow(back(0, q))
+    for d in range(ny - 1):
+        follow(remote(r_ref, rg_ref.at[y], ysend.at[d], yrecv.at[d], column[d]))
+    for q in range(2):
+        hand_over(0, q)
     keeps = [
-        pltpu.make_async_copy(l_ref, slot(core, z), local_sem.at[0]),
+        pltpu.make_async_copy(l_ref, lg_ref.at[core, z] if share else lg_ref.at[z], local_sem.at[0]),
         pltpu.make_async_copy(r_ref, rg_ref.at[y], local_sem.at[1]),
     ]
     for copy in keeps:
         copy.start()
-
-    def follow(copy):
-        copy.start()
-        sends.append(copy)
-
-    for t in range(fwd):
-        ahead_in(t).wait_recv()
-        if t + 1 < fwd:
-            follow(ahead(t + 1))
-        if share:
-            shifts.append(-1 - t)
-            follow(pass_on(len(shifts) - 1, -1 - t))
-        if t < bwd:
-            back_in(t).wait_recv()
-            if t + 1 < bwd:
-                follow(back(t + 1))
-            if share:
-                shifts.append(1 + t)
-                follow(pass_on(len(shifts) - 1, 1 + t))
+    for t in range(long):
+        for q in range(2):
+            if t < fwd[q]:
+                ahead_in(t, q).wait_recv()
+                if t + 1 < fwd[q]:
+                    follow(ahead(t + 1, q))
+                hand_over(-1 - t, q)
+            if t < bwd[q]:
+                back_in(t, q).wait_recv()
+                if t + 1 < bwd[q]:
+                    follow(back(t + 1, q))
+                hand_over(1 + t, q)
     for d in range(ny - 1):
         remote(r_ref, rg_ref.at[lax.rem(y + ny - 1 - d, ny)], ysend.at[d], yrecv.at[d], column[d]).wait_recv()
-    if share:
-        for i, shift in enumerate(shifts):
-            remote(l_ref, slot(1 - core, at(shift)), ssend.at[i], srecv.at[i], twin).wait_recv()
+    for q in range(2):
+        for i, shift in enumerate(shifts[q]):
+            remote(held(0, q), slot(1 - core, at(shift), q), ssend.at[q, i], srecv.at[q, i], twin).wait_recv()
     for copy in sends:
         copy.wait_send()
     for copy in keeps:
@@ -167,6 +180,7 @@
 
 def gather_blocks(left, right, ny, nz, share, ident, name):
     sems = lambda n: pltpu.SemaphoreType.DMA((n,))
+    pairs = pltpu.SemaphoreType.DMA((2, nz))
     lead = (2, nz) if share else (nz,)
     return pl.pallas_call(
         functools.partial(block_kernel, ny, nz, share),
@@ -176,7 +190,7 @@
             jax.ShapeDtypeStruct(lead + left.shape, left.dtype),
             jax.ShapeDtypeStruct((ny,) + right.shape, right.dtype),
         ],
-        scratch_shapes=[sems(nz), sems(nz), sems(nz), sems(nz), sems(ny), sems(ny), sems(nz), sems(nz), sems(2)],
+        scratch_shapes=[pairs] * 4 + [sems(ny)] * 2 + [pairs] * 2 + [sems(2)],
         compiler_params=pltpu.CompilerParams(collective_id=ident, has_side_effects=True),
         name=name,
     )(left, right)

time: 188 us -> 182 us (0.968)
  Pallas kernels: 128 us -> 122 us
    pallas_call x2, Pallas kernels: 54.5 us -> 51.3 us  [gather_blocks(): pl.pallas_call(functools.partial(block_kernel, ny, nz, share), in_specs=[...]
    pallas_call x1, Pallas kernels: 12.9 us -> 10.5 us  [scatter(): pl.pallas_call(functools.partial(scatter_kernel, count, number, peer_of,...]
  transfers between devices with their start and end apart: 3 -> 3, of which waited for: 1 -> 1; matrix products, arithmetic and copies ran while one was open for 6% -> 7% of each run, Pallas kernels for 7% -> 6%
where the time goes in v5:
time: 182 us; the launch traced here: 181 us
  Pallas kernels  122 us (67%)
  local copies, waits for them, and re-layouts  35.9 us (20%)
  other arithmetic  8.71 us (5%)
  matrix products  7.6 us (4%)
  starting transfers between devices  5.2 us (3%)
    pallas_call x2, Pallas kernels, gather_blocks(): pl.pallas_call(functools.partial(block_kernel, ny, nz, share), in_specs=[...  51.3 us
    pallas_call x1, Pallas kernels, column_stage(): pl.pallas_call(functools.partial(column_kernel, heads, number), in_specs=...  47.6 us
    pallas_call x1, Pallas kernels, outer_stage(): pl.pallas_call(functools.partial(outer_kernel, nz), in_specs=[vmem] * 4,...  12.3 us
    pallas_call x1, Pallas kernels, scatter(): pl.pallas_call(functools.partial(scatter_kernel, count, number, peer_of,...  10.5 us
    unnamed x38, local copies, waits for them, and re-layouts  7.88 us
    ppermute x3, starting transfers between devices, swap(): return lax.ppermute(a, 'branch', SWAP)  5.2 us
    dot_general x2, matrix products, share_of(): jnp.einsum('cik,cjk->cij', tri_left, chosen, preferred_element_type=f32)  4.39 us
    reshape x1, local copies, waits for them, and re-layouts, body(): left_rows.transpose(3, 1, 0, 2, 4).reshape(chans * rows_i, depth)  4.01 us
  transfers between devices with their start and end apart: 3, of which 1 were waited for; matrix products, arithmetic and copies ran while one was open for 7% of the time, Pallas kernels for 6%

profile of v5, /device:TPU:1, one launch (start us, length us, event | category | flops | bytes accessed | tf_op | source)
XLA Modules:
  0.0 181.3 jit_solution(3973148548559705406)
XLA Ops:
  0.7 2.6 %reshape.274 = bf16[16,32,2,4,256]{4,3,2,1,0:T(4,128)(2,1)S(1)} reshape(bf16[16,256,256]{2,1,0:T(8,128)(2,1)} %param.16) | data formatting | bytes 4194304 | tf_op jit(solution)/shard_map/reshape | solution.py:461
  3.3 0.4 constant_dynamic-slice_fusion.6
  3.7 1.6 copy.164
  5.4 0.3 copy.93
  5.7 0.7 pad.4.msend_ref
  6.4 0.6 broadcast_in_dim.8.refs_4_
  7.0 47.6 %column_attention.1 = (bf16[4,512,256]{2,1,0:T(8,128)(2,1)}, bf16[136,512]{1,0:T(8,128)(2,1)}, bf16[136,512]{1,0:T(8,128)(2,1)}, bf16[2,512,128]{2,1,0:T(8,128)(...) custom-call(bf16[4,32,16,256]{3,2,1,0:T(8,128)(2,1)} %bitcast.152, ...), custom_call_target="tpu_custom_call" | custom-call | tf_op jit(solution)/shard_map/column_attention/pallas_call | solution.py:325
  54.6 25.5 %panel_gather.1 = (bf16[2,8,136,512]{3,2,1,0:T(8,128)(2,1)}, bf16[4,136,512]{2,1,0:T(8,128)(2,1)}) custom-call(bf16[136,512]{1,0:T(8,128)(2,1)} %get-tuple-element.15.l_ref, bf16[136,512]{1,0:T(8,128)(2,1)} %get-tuple-element.16.r_ref), custom_call_target="tpu_custom_call" | custom-call | tf_op jit(solution)/shard_map/panel_gather/pallas_call | solution.py:185
  80.1 0.9 slice_bitcast_fusion
  81.0 1.8 slice.24
  82.9 0.8 slice.26
  83.7 2.9 %copy.163 = bf16[2,8,4,32,512]{4,2,0,1,3:T(4,128)(2,1)} copy(bf16[2,8,4,32,512]{4,3,2,1,0:T(8,128)(2,1)S(1)} %bitcast.148) | data formatting | bytes 4194304 | tf_op jit(solution)/shard_map/reshape | solution.py:514
  86.6 4.0 %reshape.281.left_ref = bf16[2048,512]{1,0:T(8,128)(2,1)} reshape(bf16[32,8,2,4,512]{4,3,2,1,0:T(4,128)(2,1)} %bitcast.149) | data formatting | bytes 4194304 | tf_op jit(solution)/shard_map/reshape | solution.py:515
  90.7 0.2 copy.100
  90.9 0.7 copy.165
  91.6 0.8 fusion.9.inv_ref
  92.4 12.3 %outer_product.1 = bf16[8,16,8,128]{3,2,1,0:T(8,128)(2,1)} custom-call(bf16[2048,512]{1,0:T(8,128)(2,1)} %reshape.281.left_ref, bf16[4,136,512]{2,1,0:T(8,128)(2,1)} %get-tuple-element.18.right_ref, f32[64,16]{1,0:T(8,128)} %fusion.9.inv_ref, bf16[512,256]{1,0:T(8,128)(2,1)} %bitcast.156), custom_call_target="tpu_custom_call" | custom-call | tf_op jit(solution)/shard_map/outer_product/pallas_call | solution.py:407
  104.7 1.0 convert_element_type.161
  105.7 0.5 convert_reduce_fusion
  106.3 0.8 fusion.12
  107.1 0.6 fusion.14
  107.8 0.4 fusion.31
  108.2 1.0 fusion.30
  109.4 0.2 copy.127
  109.9 1.3 copy.129
  111.8 1.1 fusion.27
  112.9 25.8 %triangle_gather.1 = (bf16[8,128,8,128]{3,2,1,0:T(8,128)(2,1)}, bf16[4,128,8,128]{3,2,1,0:T(8,128)(2,1)}) custom-call(bf16[128,8,128]{2,1,0:T(8,128)(2,1)} %get-tuple-element.49.l_ref, bf16[128,8,128]{2,1,0:T(8,128)(2,1)} %get-tuple-element.48.r_ref), custom_call_target="tpu_custom_call" | custom-call | tf_op jit(solution)/shard_map/triangle_gather/pallas_call | solution.py:185
  138.7 2.6 %copy.111 = bf16[4,128,2,4,128]{4,1,3,0,2:T(8,128)(2,1)} copy(bf16[4,128,2,4,128]{4,3,2,1,0:T(4,128)(2,1)} %bitcast.159) | data formatting | bytes 2097152 | tf_op jit(solution)/shard_map/reshape | solution.py:544
  141.3 2.1 %constant_dynamic-slice_fusion.1 = (bf16[1,128,16,128]{3,1,2,0:T(8,128)(2,1)S(1)}, bf16[1,128,16,128]{3,1,2,0:T(8,128)(2,1)}) fusion(bf16[2,128,16,128]{3,1,2,0:T(8,128)(2,1)} %bitcast.153, s32[]{:T(128)S(6)} %select_n.76, s32[]{:T(128)S(6)} %select_n.71), kind=kLoop, calls=%fused_computation.61 | loop fusion | bytes 2097160 | tf_op jit(solution)/shard_map/jit(dynamic_index_in_dim)/dynamic_slice | solution.py:547
  143.4 2.2 %fusion = f32[128,64,16]{1,2,0:T(8,128)} fusion(bf16[1,128,16,128]{3,1,2,0:T(8,128)(2,1)S(1)} %get-tuple-element.44, bf16[8,128,8,128]{3,2,1,0:T(8,128)(2,1)S(1)} %copy-done.1), kind=kOutput, calls=%fused_computation.1 | convolution fusion | flops 33554432 | bytes 3145728 | tf_op jit(solution)/shard_map/cik,cjk->cij/dot_general | solution.py:548
  145.6 2.5 %copy.114 = f32[128,64,16]{0,2,1:T(8,128)} copy(f32[128,64,16]{1,2,0:T(8,128)} %fusion) | data formatting | bytes 1048576 | tf_op jit(solution)/shard_map/cik,cjk->cij/dot_general | solution.py:548
  148.1 3.8 %collective-permute-start.1 = (f32[128,64,16]{0,2,1:T(8,128)}, f32[128,64,16]{0,2,1:T(8,128)}, u32[]{:S(2)}, u32[]{:S(2)}) collective-permute-start(f32[128,64,16]{0,2,1:T(8,128)} %copy.114), channel_id=1, source_target_pairs={{0,128},{128,0},{1,129},{129,1},{2,130},{130,2},{3,131},{131,3},{4... | collective-permute-start | bytes 1572872 | tf_op jit(solution)/shard_map/ppermute | solution.py:452
  151.9 0.9 fusion.25
  152.8 0.7 slice_reduce_fusion
  153.6 1.1 fusion.8
  154.7 2.2 %fusion.2 = f32[128,64,16]{1,2,0:T(8,128)} fusion(bf16[1,128,16,128]{3,1,2,0:T(8,128)(2,1)S(1)} %copy-done.3, bf16[8,128,8,128]{3,2,1,0:T(8,128)(2,1)S(1)} %copy-done.1), kind=kOutput, calls=%fused_computation.3 | convolution fusion | flops 33554432 | bytes 3145728 | tf_op jit(solution)/shard_map/cik,cjk->cij/dot_general | solution.py:548
  156.9 1.7 copy.115
  159.3 0.6 copy.116
  159.9 0.9 convolution_convert_fusion
  160.8 10.5 %triangle_exchange.1 = bf16[8,8,16,128]{3,2,1,0:T(8,128)(2,1)} custom-call(bf16[8,8,16,128]{3,2,1,0:T(8,128)(2,1)} %bitcast.162), custom_call_target="tpu_custom_call" | custom-call | tf_op jit(solution)/shard_map/triangle_exchange/pallas_call | solution.py:76
  171.3 1.0 convert_bitcast_fusion
  172.7 1.4 collective-permute-start.2
  174.1 1.2 collective-permute-done.2
  175.4 0.3 copy.118
  175.8 0.3 copy.119
  176.2 1.0 copy.121
  177.2 1.4 broadcast_select_fusion.1
  178.8 2.5 %copy.120 = bf16[512,8,256]{2,1,0:T(8,128)(2,1)} copy(bf16[512,8,256]{2,0,1:T(8,128)(2,1)S(1)} %maximum_bitcast_fusion) | data formatting | bytes 4194304
  (64 shorter events, 3.1 us)
Async XLA Ops:
  0.6 105.1 %copy-start = (bf16[8,256,128]{2,1,0:T(8,128)(2,1)S(1)}, bf16[8,256,128]{2,1,0:T(8,128)(2,1)}, u32[]{:S(2)}) copy-start(bf16[8,256,128]{2,1,0:T(8,128)(2,1)} %param.19) | copy-start | bytes 1572868
  3.3 2.0 %copy-start.10 = (s32[16,256]{1,0:T(8,128)S(1)}, s32[16,256]{1,0:T(8,128)}, u32[]{:S(2)}) copy-start(s32[16,256]{1,0:T(8,128)} %param.17) | copy-start | bytes 49156
  3.3 2.0 %copy-start.11 = (s32[256]{0:T(256)S(1)}, s32[256]{0:T(256)}, u32[]{:S(2)}) copy-start(s32[256]{0:T(256)} %param.18) | copy-start | bytes 3076
  3.3 3.1 %copy-start.12 = (f32[64]{0:T(128)S(1)}, f32[64]{0:T(128)}, u32[]{:S(2)}) copy-start(f32[64]{0:T(128)} %param.30) | copy-start | bytes 772
  86.6 4.0 %copy-start.7 = (bf16[2,512,128]{2,1,0:T(8,128)(2,1)S(1)}, bf16[2,512,128]{2,1,0:T(8,128)(2,1)}, u32[]{:S(2)}) copy-start(bf16[2,512,128]{2,1,0:T(8,128)(2,1)} %get-tuple-element.19) | copy-start | bytes 786436
  104.7 2.4 %copy-start.8 = (bf16[2,4,64,128]{3,2,1,0:T(8,128)(2,1)S(1)}, bf16[2,4,64,128]{3,2,1,0:T(8,128)(2,1)}, u32[]{:S(2)}) copy-start(bf16[2,4,64,128]{3,2,1,0:T(8,128)(2,1)} %get-tuple-element.21) | copy-start | bytes 393220
  104.7 2.4 %copy-start.13 = (f32[128]{0:T(128)S(1)}, f32[128]{0:T(128)}, u32[]{:S(2)}) copy-start(f32[128]{0:T(128)} %param.27) | copy-start | bytes 1540
  138.7 4.7 %copy-start.1 = (bf16[8,128,8,128]{3,2,1,0:T(8,128)(2,1)S(1)}, bf16[8,128,8,128]{3,2,1,0:T(8,128)(2,1)}, u32[]{:S(2)}) copy-start(bf16[8,128,8,128]{3,2,1,0:T(8,128)(2,1)} %get-tuple-element.22) | copy-start | bytes 6291460
  145.6 8.0 %copy-start.14 = (bf16[2,64,128]{2,1,0:T(8,128)(2,1)S(1)}, bf16[2,64,128]{2,1,0:T(8,128)(2,1)}, u32[]{:S(2)}) copy-start(bf16[2,64,128]{2,1,0:T(8,128)(2,1)} %get-tuple-element.20) | copy-start | bytes 98308
  148.1 8.8 %collective-permute-start.1 = (f32[128,64,16]{0,2,1:T(8,128)}, f32[128,64,16]{0,2,1:T(8,128)}, u32[]{:S(2)}, u32[]{:S(2)}) collective-permute-start(f32[128,64,16]{0,2,1:T(8,128)} %copy.114), channel_id=1, source_target_pairs={{0,128},{128,0},{1,129},{129,1},{2,130},{130,2},{3,131},{131,3},{4... | collective-permute-start | bytes 1572872 | tf_op jit(solution)/shard_map/ppermute | solution.py:452
  151.9 25.3 %collective-permute-start = (bf16[4,512,256]{2,1,0:T(8,128)(2,1)}, bf16[4,512,256]{2,1,0:T(8,128)(2,1)}, u32[]{:S(2)}, u32[]{:S(2)}) collective-permute-start(bf16[4,512,256]{2,1,0:T(8,128)(2,1)} %get-tuple-element.14), channel_id=1, source_target_pairs={{0,128},{128,0},{1,129},{129,1},{2,130},{130,2},{3,131},{131,3},{4... | collective-permute-start | bytes 3145736 | tf_op jit(solution)/shard_map/ppermute | solution.py:452
  153.6 1.1 copy-start.3
  156.9 1.7 copy-start.2
  158.8 1.1 copy-start.9
  159.2 13.1 %copy-start.4 = (f32[8,4,8,4,128]{4,3,1,2,0:T(4,128)S(1)}, f32[8,4,8,4,128]{4,3,1,2,0:T(4,128)}, u32[]{:S(2)}) copy-start(f32[8,4,8,4,128]{4,3,1,2,0:T(4,128)} %fusion.25) | copy-start | bytes 1572868
  159.3 13.1 %copy-start.6 = (f32[1024,128]{1,0:T(8,128)S(1)}, f32[1024,128]{1,0:T(8,128)}, u32[]{:S(2)}) copy-start(f32[1024,128]{1,0:T(8,128)} %fusion.8) | copy-start | bytes 1572868
  172.7 4.6 %copy-start.5 = (bf16[4,512,256]{2,1,0:T(8,128)(2,1)S(1)}, bf16[4,512,256]{2,1,0:T(8,128)(2,1)}, u32[]{:S(2)}) copy-start(bf16[4,512,256]{2,1,0:T(8,128)(2,1)} %get-tuple-element.14) | copy-start | bytes 3145732
  172.7 2.5 %collective-permute-start.2 = (bf16[8,128,64]{2,1,0:T(8,128)(2,1)S(1)}, bf16[8,128,64]{2,1,0:T(8,128)(2,1)S(1)}, u32[]{:S(2)}, u32[]{:S(2)}) collective-permute-start(bf16[8,128,64]{2,1,0:T(8,128)(2,1)S(1)} %constant_dynamic-slice_fusion), channel_id=1, source_target_pairs={{0,128},{128,0},{1,129},{129,1},{2,130},{130,2},{3,131},{131,3},{4... | collective-permute-start | bytes 393224 | tf_op jit(solution)/shard_map/ppermute | solution.py:452
